TPU v7x, 256 devices: a whole 4x4x8 slice. The times are simulated.
256 devices in a mesh: chan: 64 (over x, y_hi, z), band: 4 (over y_lo, core).
Axes of the slice: x: 4, y: 4 (y_hi: 2, y_lo: 2; y = y_hi * 2 + y_lo), z: 8, core: 2. Of those that a mesh axis runs over, the one named last changes fastest.
Arguments:
- spectra: float32 [2, 32, 96, 8192], P(None, None, 'band', 'chan'), may hold values from -6 to 6
- taps: float32 [96, 16], replicated, may hold values from -2.5 to 2.5
Outputs:
- stacked: bfloat16 [8, 2, 8192, 8192], P('band', None, 'chan')
All inputs are finite; a program needn't handle non-finite values.
Results may differ from a plain program's by a relative error of at most 0.0057.
Values may be sent and summed in bfloat16 or wider, within the bound.
No kernel may reach another device: no remote copies, remote signals or barrier semaphores. Data moves between devices by JAX's collectives and lax.ppermute only.
A program may use at most 192 MiB of HBM per device.

v0:
```python
import jax
import jax.numpy as jnp
from jax import lax
from jax.sharding import PartitionSpec as P

TAPS = 16
SMOOTH = 5
BAND_BINS = 12


water_level = 0.1


def padded(shard, sides, width, wrap):
    for axis, dim in sides:
        devices, length = (lax.axis_size(axis), shard.shape[dim])
        up = [(i, (i + 1) % devices) for i in range(devices if wrap else devices - 1)]
        down = [(j, i) for i, j in up]
        last = lax.slice_in_dim(shard, length - width, length, axis=dim)
        first = lax.slice_in_dim(shard, 0, width, axis=dim)
        before = lax.ppermute(last, axis, up)
        after = lax.ppermute(first, axis, down)
        shard = jnp.concatenate([before, shard, after], axis=dim)
    return shard


def fan_filter(extended, coeffs, width):
    result = jnp.zeros(extended.shape[:-1] + (width,), jnp.float32)
    for tap_index in range(coeffs.shape[1]):
        result = (
            result + coeffs[:, tap_index][:, None] * extended[..., tap_index : tap_index + width]
        )
    return result


def whiten(filtered, amp_ext, local_bins):
    smoothed = jnp.zeros(filtered.shape[1:], jnp.float32)
    for offset in range(SMOOTH):
        smoothed = smoothed + amp_ext[:, offset : offset + local_bins, :]
    smoothed = smoothed / SMOOTH
    return (filtered / (smoothed + water_level)[None]).astype(jnp.bfloat16)


def arrange(whitened, band_count):
    shaped = whitened.reshape(2, whitened.shape[1], band_count, BAND_BINS, whitened.shape[3])
    shaped = shaped.transpose(2, 0, 1, 3, 4)
    return shaped.reshape(band_count, 2 * whitened.shape[1] * BAND_BINS, whitened.shape[3])


def partner(whitened):
    return jnp.concatenate([-whitened[1:2], whitened[0:1]], axis=0)


def body(spectra, taps):
    half_taps = TAPS // 2
    reach = SMOOTH // 2
    local_bins = spectra.shape[2]
    local_chan = spectra.shape[3]
    anchor = lax.axis_index("band") * local_bins
    padded_taps = jnp.pad(taps, ((reach, reach), (0, 0)))
    coeffs = lax.dynamic_slice_in_dim(padded_taps, anchor + reach, local_bins, 0)
    extended = padded(spectra, (("chan", 3),), half_taps, True)
    filtered = fan_filter(extended, coeffs, local_chan)
    amplitude = jnp.sqrt(filtered[0] * filtered[0] + filtered[1] * filtered[1])
    amp_ext = padded(amplitude, (("band", 1),), reach, False)
    whitened = whiten(filtered, amp_ext, local_bins)
    band_count = local_bins // BAND_BINS
    features = arrange(whitened, band_count)
    scale_factor = 1.0 / (whitened.shape[1] * BAND_BINS)
    remote = lax.all_gather(whitened, "chan", axis=3, tiled=True)
    right = arrange(remote, band_count)
    turned = arrange(partner(remote), band_count)
    real_part = jnp.einsum("bki,bkj->bij", features, right, preferred_element_type=jnp.float32)
    imag_part = jnp.einsum("bki,bkj->bij", features, turned, preferred_element_type=jnp.float32)
    return (jnp.stack([real_part, imag_part], axis=1) * scale_factor).astype(jnp.bfloat16)


def solution(mesh):
    placed = (P(None, None, "band", "chan"), P())
    return jax.shard_map(
        body, mesh=mesh, in_specs=placed, out_specs=P("band", None, "chan", None), check_vma=False
    )
```

profile of v0, /device:TPU:8, one launch (start us, length us, event | category | flops | bytes accessed | tf_op | source)
XLA Modules:
  0.0 518.0 jit_solution(13013517061511016048)
XLA Ops:
  6.5 1.6 fusion.81
  8.4 9.8 %collective-permute-start.1 = (f32[2,32,24,8]{1,3,2,0:T(8,128)S(1)}, f32[2,32,24,8]{1,3,2,0:T(8,128)S(1)}, u32[]{:S(2)}, u32[]{:S(2)}) collective-permute-start(f32[2,32,24,8]{1,3,2,0:T(8,128)S(1)} %copy.36), channel_id=1, source_target_pairs={{4,0},{8,4},{12,8},{16,12},{20,16},{24,20},{28,24},{32,28},{36,32}... | collective-permute-start | bytes 147464 | tf_op jit(solution)/shard_map/ppermute | solution.py:22
  18.6 1.1 fusion.66
  19.6 1.0 fusion.67
  20.7 1.3 copy.22
  21.9 8.7 %collective-permute-done = f32[2,32,24,8]{1,3,2,0:T(8,128)S(1)} collective-permute-done((f32[2,32,24,8]{1,3,2,0:T(8,128)S(1)}, f32[2,32,24,8]{1,3,2,0:T(8,128)S(1)}, u32[]{:S(2)}, u32[]{:S(2)}) %collective-permute-start) | collective-permute-done | bytes 49184 | tf_op jit(solution)/shard_map/ppermute | solution.py:21
  30.6 0.3 copy.21
  31.0 0.3 copy.26
  31.2 6.6 %fusion.14 = f32[2,32,24,128]{3,1,2,0:T(8,128)S(1)} fusion(f32[2,32,24,128]{3,1,2,0:T(8,128)S(1)} %copy.22, f32[2,32,24,8]{3,1,2,0:T(8,128)S(1)} %copy.26, f32[2,32,24,8]{3,1,2,0:T(8,128)S(1)} %copy.21, f32[24]{0:T(128)S(1)} %get-tuple-element.26, f32[24]{0:T(128)S(1)} %get-tuple-element.12, f32[24]{0:T(128)S(1)} %get-tuple-element.13, ...), kind=kLoop, calls=%fused_computation.39 | loop fusion | flops 9043968 | bytes 1672704 | tf_op jit(solution)/shard_map/add | solution.py:31
  38.0 1.9 collective-permute-start.2
  39.9 3.6 collective-permute-start.3
  43.6 1.6 collective-permute-done.3
  45.2 0.9 divide_convert_fusion
  46.1 1.4 copy.27
  47.5 0.4 copy.29
  48.0 227.1 %all-gather.2.cloned.1.call-done = bf16[2,32,24,8192]{3,1,2,0:T(8,128)(2,1)} async-done(((bf16[2,32,24,128]{3,1,2,0:T(8,128)(2,1)}), bf16[2,32,24,8192]{3,1,2,0:T(8,128)(2,1)}) %all-gather.2.cloned.1.call-update) | async-done | bytes 25165840 | tf_op jit(solution)/shard_map/all_gather | solution.py:70
  275.1 46.2 %copy.28 = bf16[2,2,32,12,8192]{4,0,3,2,1:T(2,128)(2,1)} copy(bf16[2,2,32,12,8192]{4,2,3,0,1:T(8,128)(2,1)} %bitcast.52) | data formatting | bytes 50331648 | tf_op jit(solution)/shard_map/transpose | solution.py:46
  321.4 8.7 %slice_negate_fusion = (bf16[1,32,24,8192]{3,1,2,0:T(8,128)(2,1)}, bf16[1,32,24,8192]{3,1,2,0:T(8,128)(2,1)}) fusion(bf16[2,32,24,8192]{3,1,2,0:T(8,128)(2,1)S(1)} %bitcast.54), kind=kLoop, calls=%fused_computation.7 | loop fusion | flops 6291456 | bytes 50331648 | tf_op jit(solution)/shard_map/neg | solution.py:51
  330.1 11.8 %pad_maximum_fusion = bf16[2,32,24,8192]{3,1,2,0:T(8,128)(2,1)S(1)} fusion(bf16[1,32,24,8192]{3,1,2,0:T(8,128)(2,1)} %get-tuple-element.6, bf16[1,32,24,8192]{3,1,2,0:T(8,128)(2,1)} %get-tuple-element.5), kind=kLoop, calls=%fused_computation | loop fusion | flops 12582912 | bytes 50331648 | tf_op jit(solution)/shard_map/concatenate | solution.py:51
  341.9 53.3 %copy.31 = bf16[2,2,32,12,8192]{4,0,3,2,1:T(2,128)(2,1)} copy(bf16[2,2,32,12,8192]{4,2,3,0,1:T(8,128)(2,1)S(1)} %bitcast.57) | data formatting | bytes 50331648 | tf_op jit(solution)/shard_map/transpose | solution.py:46
  395.2 56.0 %fusion.5 = f32[2,1,128,8192]{3,2,0,1:T(8,128)S(1)} fusion(bf16[2,768,128]{1,2,0:T(8,128)(2,1)S(1)} %copy.29, bf16[2,768,8192]{2,0,1:T(2,128)(2,1)} %bitcast.55), kind=kOutput, calls=%fused_computation.8 | convolution fusion | flops 3221225472 | bytes 33947648 | tf_op jit(solution)/shard_map/bki,bkj->bij/dot_general | solution.py:73
  451.2 44.2 %fusion.8 = f32[2,1,128,8192]{3,2,0,1:T(8,128)} fusion(bf16[2,768,128]{1,2,0:T(8,128)(2,1)S(1)} %copy.29, bf16[2,768,8192]{2,0,1:T(2,128)(2,1)} %bitcast.56), kind=kOutput, calls=%fused_computation.9 | convolution fusion | flops 3221225472 | bytes 33947648 | tf_op jit(solution)/shard_map/bki,bkj->bij/dot_general | solution.py:74
  495.4 7.8 %fusion.4 = bf16[2,2,128,8192]{3,2,0,1:T(8,128)(2,1)} fusion(f32[2,1,128,8192]{3,2,0,1:T(8,128)} %fusion.8, f32[2,1,128,8192]{3,2,0,1:T(8,128)S(1)} %fusion.5), kind=kLoop, calls=%fused_computation.6 | loop fusion | flops 12582912 | bytes 25165824 | tf_op jit(solution)/shard_map/convert_element_type | solution.py:75
  503.2 7.8 %copy.34 = bf16[2,2,128,8192]{3,2,1,0:T(8,128)(2,1)} copy(bf16[2,2,128,8192]{3,2,0,1:T(8,128)(2,1)} %fusion.4) | data formatting | bytes 16777216 | tf_op jit(solution)/shard_map/convert_element_type | solution.py:75
  (23 shorter events, 0.8 us)
Async XLA Ops:
  6.5 268.6 %all-gather.2.cloned.1.call-start = ((), (), s32[]{:S(2)}) async-start(), calls=%async_computation | async-start | bytes 25559040 | tf_op jit(solution)/shard_map/all_gather | solution.py:70
  8.4 22.5 %collective-permute-start.1 = (f32[2,32,24,8]{1,3,2,0:T(8,128)S(1)}, f32[2,32,24,8]{1,3,2,0:T(8,128)S(1)}, u32[]{:S(2)}, u32[]{:S(2)}) collective-permute-start(f32[2,32,24,8]{1,3,2,0:T(8,128)S(1)} %copy.36), channel_id=1, source_target_pairs={{4,0},{8,4},{12,8},{16,12},{20,16},{24,20},{28,24},{32,28},{36,32}... | collective-permute-start | bytes 147464 | tf_op jit(solution)/shard_map/ppermute | solution.py:22
  18.5 12.1 %collective-permute-start = (f32[2,32,24,8]{1,3,2,0:T(8,128)S(1)}, f32[2,32,24,8]{1,3,2,0:T(8,128)S(1)}, u32[]{:S(2)}, u32[]{:S(2)}) collective-permute-start(f32[2,32,24,8]{1,3,2,0:T(8,128)S(1)} %copy.35), channel_id=1, source_target_pairs={{0,4},{4,8},{8,12},{12,16},{16,20},{20,24},{24,28},{28,32},{32,36}... | collective-permute-start | bytes 147464 | tf_op jit(solution)/shard_map/ppermute | solution.py:21
  38.0 5.6 %collective-permute-start.2 = (f32[32,2,128]{2,0,1:T(8,128)S(1)}, f32[32,2,128]{2,0,1:T(8,128)S(1)}, u32[]{:S(2)}, u32[]{:S(2)}) collective-permute-start(f32[32,2,128]{2,0,1:T(8,128)S(1)} %get-tuple-element.9), channel_id=1, source_target_pairs={{0,1},{1,2},{2,3},{4,5},{5,6},{6,7},{8,9},{9,10},{10,11},{12,13},{... | collective-permute-start | bytes 98312 | tf_op jit(solution)/shard_map/ppermute | solution.py:21
  39.9 5.2 %collective-permute-start.3 = (f32[32,2,128]{2,0,1:T(8,128)S(1)}, f32[32,2,128]{2,0,1:T(8,128)S(1)}, u32[]{:S(2)}, u32[]{:S(2)}) collective-permute-start(f32[32,2,128]{2,0,1:T(8,128)S(1)} %get-tuple-element.10), channel_id=1, source_target_pairs={{1,0},{2,1},{3,2},{5,4},{6,5},{7,6},{9,8},{10,9},{11,10},{13,12},{... | collective-permute-start | bytes 98312 | tf_op jit(solution)/shard_map/ppermute | solution.py:22
  275.1 46.2 %slice-start = ((s8[25165824]{0:T(1024)(128)(4,1)}), s8[4194304]{0:T(1024)(128)(4,1)S(1)}, s32[]{:S(2)}) async-start(s8[25165824]{0:T(1024)(128)(4,1)} %bitcast.53), calls=%async_computation.1 | async-start | bytes 8388608
  275.1 46.2 %slice-start.1 = ((s8[25165824]{0:T(1024)(128)(4,1)}), s8[4194304]{0:T(1024)(128)(4,1)S(1)}, s32[]{:S(2)}) async-start(s8[25165824]{0:T(1024)(128)(4,1)} %bitcast.53), calls=%async_computation.2 | async-start | bytes 8388608
  275.1 46.2 %slice-start.2 = ((s8[25165824]{0:T(1024)(128)(4,1)}), s8[4194304]{0:T(1024)(128)(4,1)S(1)}, s32[]{:S(2)}) async-start(s8[25165824]{0:T(1024)(128)(4,1)} %bitcast.53), calls=%async_computation.3 | async-start | bytes 8388608
  275.1 46.2 %slice-start.3 = ((s8[25165824]{0:T(1024)(128)(4,1)}), s8[4194304]{0:T(1024)(128)(4,1)S(1)}, s32[]{:S(2)}) async-start(s8[25165824]{0:T(1024)(128)(4,1)} %bitcast.53), calls=%async_computation.4 | async-start | bytes 8388608
  275.1 46.3 %slice-start.4 = ((s8[25165824]{0:T(1024)(128)(4,1)}), s8[4194304]{0:T(1024)(128)(4,1)S(1)}, s32[]{:S(2)}) async-start(s8[25165824]{0:T(1024)(128)(4,1)} %bitcast.53), calls=%async_computation.5 | async-start | bytes 8388608
  275.1 46.3 %slice-start.5 = ((s8[25165824]{0:T(1024)(128)(4,1)}), s8[4194304]{0:T(1024)(128)(4,1)S(1)}, s32[]{:S(2)}) async-start(s8[25165824]{0:T(1024)(128)(4,1)} %bitcast.53), calls=%async_computation.6 | async-start | bytes 8388608
Sparse Core Ops, SparseCore 0:
  46.3 228.7 all-gather.1
where the time goes:
time: 525 us; the launch traced here: 518 us
  waiting for transfers between devices  237 us (45%)
  local copies, waits for them, and re-layouts  115 us (22%)
  matrix products  100 us (19%)
  other arithmetic  35.9 us (7%)
  starting transfers between devices  15.4 us (3%)
  between operations  13.8 us (3%)
    all_gather x1, waiting for transfers between devices, body(): remote = lax.all_gather(whitened, 'chan', axis=3, tiled=True)  227 us
    transpose x3, local copies, waits for them, and re-layouts, arrange(): shaped = shaped.transpose(2, 0, 1, 3, 4)  101 us
    dot_general x1, matrix products, body(): jnp.einsum('bki,bkj->bij', features, right, preferred_element_type=jnp.fl...  56 us
    dot_general x1, matrix products, body(): jnp.einsum('bki,bkj->bij', features, turned, preferred_element_type=jnp.f...  44.2 us
    ppermute x2, starting transfers between devices, padded(): after = lax.ppermute(first, axis, down)  13.5 us
    concatenate x1, other arithmetic, partner(): return jnp.concatenate([-whitened[1:2], whitened[0:1]], axis=0)  11.8 us
  transfers between devices with their start and end apart: 5, of which 3 were waited for; matrix products, arithmetic and copies ran while one was open for 1% of the time, Pallas kernels for 0%

commit v1 on v0

v1 whole, which is shorter than its diff:
```python
import functools

import jax
import jax.numpy as jnp
from jax import lax
from jax.experimental import pallas as pl
from jax.experimental.pallas import tpu as pltpu
from jax.sharding import Mesh, PartitionSpec as P


TAPS = 16
SMOOTH = 5
BAND_BINS = 12
AXES = ("x", "yh", "z", "yl", "core")
SIZES = (4, 2, 8, 2, 2)
CHAN = ("x", "yh", "z")
BAND = ("yl", "core")
BLK = 128
water_level = 0.1


def shifted(dx=0, dy=0, dz=0):
    pairs = []
    for i in range(256):
        core, yl, z, yh, x = i % 2, i // 2 % 2, i // 4 % 8, i // 32 % 2, i // 64
        y = (yh * 2 + yl + dy) % 4
        x, z = (x + dx) % 4, (z + dz) % 8
        pairs.append((i, (((x * 2 + y // 2) * 8 + z) * 2 + y % 2) * 2 + core))
    return pairs


def move(value, **delta):
    return lax.ppermute(value, AXES, shifted(**delta))


def neighbours(axes, wrap):
    devices = lax.axis_size(axes)
    up = [(i, (i + 1) % devices) for i in range(devices if wrap else devices - 1)]
    return up, [(j, i) for i, j in up]


def filter_body(x_ref, before_ref, after_ref, taps_ref, filt_ref, amp_ref):
    bins, taps = x_ref.shape[1], TAPS
    start = (lax.axis_index("yl") * 2 + lax.axis_index("core")) * bins
    lanes = lax.broadcasted_iota(jnp.int32, x_ref.shape[2:], 1)

    def one_bin(f, carry):
        power = None
        for k in range(2):
            x = x_ref[k, f]
            gap = jnp.zeros((x.shape[0], BLK - taps), jnp.float32)
            halo = jnp.concatenate([after_ref[k, f], gap, before_ref[k, f]], axis=1)
            total = jnp.zeros_like(x)
            for t in range(taps):
                lag = t - taps // 2
                if lag == 0:
                    shifted_x = x
                else:
                    inside = lanes >= lag if lag > 0 else lanes < BLK + lag
                    shifted_x = pltpu.roll(jnp.where(inside, x, halo), -lag % BLK, 1)
                total = total + taps_ref[(start + f) * taps + t] * shifted_x
            filt_ref[k, f] = total
            power = total * total if power is None else power + total * total
        amp_ref[f] = jnp.sqrt(power)
        return carry

    lax.fori_loop(0, bins, one_bin, 0)


def whiten_body(filt_ref, amp_ref, below_ref, above_ref, feat_ref, ext):
    bins, reach = amp_ref.shape[0], SMOOTH // 2
    ext[:reach] = below_ref[...]
    ext[reach : reach + bins] = amp_ref[...]
    ext[reach + bins :] = above_ref[...]
    windows = amp_ref.shape[1]

    for band in range(2):

        def one_bin(f, carry):
            g = band * BAND_BINS + f
            smoothed = jnp.zeros(amp_ref.shape[1:], jnp.float32)
            for d in range(SMOOTH):
                smoothed = smoothed + ext[g + d]
            under = smoothed / SMOOTH + water_level
            for k in range(2):
                row = pl.multiple_of((k * BAND_BINS + f) * windows, windows)
                feat_ref[band, pl.ds(row, windows)] = (filt_ref[k, g] / under).astype(jnp.bfloat16)
            return carry

        lax.fori_loop(0, BAND_BINS, one_bin, 0)


def left_body(feat_ref, left_ref):
    half = feat_ref.shape[1] // 2
    for band in range(2):
        flipped = feat_ref[band].T
        left_ref[band, :BLK] = flipped
        left_ref[band, BLK:] = jnp.concatenate([flipped[:, half:], -flipped[:, :half]], axis=1)


def simple_call(kernel, outs, ins, scratch=(), smem=()):
    vmem = pl.BlockSpec(memory_space=pltpu.VMEM)
    size = sum(v.size * v.dtype.itemsize for v in (*ins, *outs))
    return pl.pallas_call(
        kernel,
        out_shape=outs,
        in_specs=[
            pl.BlockSpec(memory_space=pltpu.SMEM) if i in smem else vmem for i in range(len(ins))
        ],
        out_specs=[vmem] * len(outs),
        scratch_shapes=list(scratch),
        cost_estimate=pl.CostEstimate(flops=4 * size, bytes_accessed=size, transcendentals=0),
        compiler_params=pltpu.CompilerParams(vmem_limit_bytes=20 << 20),
    )(*ins)


def left_rows(features):
    bands, k, c = features.shape
    return simple_call(
        left_body, [jax.ShapeDtypeStruct((bands, 2 * c, k), features.dtype)], [features]
    )[0]


def features_of(spectra, taps):
    edge, reach = TAPS // 2, SMOOTH // 2
    turned = spectra.transpose(0, 2, 1, 3)
    bins, windows, chan = turned.shape[1:]
    up, down = neighbours(CHAN, True)
    last = spectra[..., chan - edge :].transpose(0, 2, 3, 1)
    first = spectra[..., :edge].transpose(0, 2, 3, 1)
    before = lax.ppermute(last, CHAN, up).swapaxes(2, 3)
    after = lax.ppermute(first, CHAN, down).swapaxes(2, 3)
    f32 = jnp.float32
    filtered, amplitude = simple_call(
        filter_body,
        [
            jax.ShapeDtypeStruct(turned.shape, f32),
            jax.ShapeDtypeStruct((bins, windows, chan), f32),
        ],
        [turned, before, after, taps.reshape(-1)],
        smem=(3,),
    )
    up, down = neighbours(BAND, False)
    below = lax.ppermute(amplitude[bins - reach :], BAND, up)
    above = lax.ppermute(amplitude[:reach], BAND, down)
    rows = 2 * windows * BAND_BINS
    return simple_call(
        whiten_body,
        [jax.ShapeDtypeStruct((bins // BAND_BINS, rows, chan), jnp.bfloat16)],
        [filtered, amplitude, below, above],
        scratch=[pltpu.VMEM((bins + 2 * reach, windows, chan), f32)],
    )[0]


def column(dx, dz, other):
    x = lax.rem(lax.axis_index("x") + (dx % 4), 4)
    yh = lax.axis_index("yh")
    yh = 1 - yh if other else yh
    z = lax.rem(lax.axis_index("z") + (dz % 8), 8)
    return pl.multiple_of(((x * 2 + yh) * 8 + z) * BLK, BLK)


def cross_body(items, scale, n_groups, first, *refs):
    own_left, pair_left = refs[:2]
    groups = refs[2 : 2 + n_groups]
    rest = refs[2 + n_groups :] if first else refs[3 + n_groups :]
    out, sent, own, sems = rest
    copies = []
    at = 0
    for k, pair in pairs_of(items):
        band, both = pair[0][2], any(item[6] for item in pair)
        right = jnp.concatenate([groups[item[0]][item[1]] for item in pair], axis=1)
        width = len(pair) * BLK
        for side in range(2 if both else 1):
            rows = (own_left, pair_left)[side][band]
            res = jnp.dot(rows, right, preferred_element_type=jnp.float32) * scale
            res = res.astype(jnp.bfloat16).reshape(2, BLK, width)
            for s, (_, _, _, dx, dz, other, send) in enumerate(pair):
                tile = res[:, :, s * BLK : (s + 1) * BLK]
                if side == 0:
                    own[k + s] = tile
                    copy = pltpu.make_async_copy(
                        own.at[k + s],
                        out.at[band, :, :, pl.ds(column(dx, dz, other), BLK)],
                        sems.at[k + s],
                    )
                    copy.start()
                    copies.append(copy)
                elif send:
                    sent[at] = tile
                    at += 1
    for copy in copies:
        copy.wait()


def pairs_of(items):
    k = 0
    while k < len(items):
        n = 2 if k + 1 < len(items) and items[k + 1][2] == items[k][2] else 1
        yield k, items[k : k + n]
        k += n


def cross(out, lefts, groups, items, scale, out_shape):
    n, n_sent = len(items), sum(item[6] for item in items)
    first = out is None
    k = lefts[0].shape[2]
    vmem = pl.BlockSpec(memory_space=pltpu.VMEM)
    hbm = pl.BlockSpec(memory_space=pl.ANY)
    return pl.pallas_call(
        functools.partial(cross_body, items, scale, len(groups), first),
        out_shape=[out_shape, jax.ShapeDtypeStruct((n_sent, 2, BLK, BLK), jnp.bfloat16)],
        in_specs=[vmem] * (2 + len(groups)) + ([] if first else [hbm]),
        out_specs=[hbm, vmem],
        scratch_shapes=[
            pltpu.VMEM((n, 2, BLK, BLK), jnp.bfloat16),
            pltpu.SemaphoreType.DMA((n,)),
        ],
        input_output_aliases={} if first else {2 + len(groups): 0},
        cost_estimate=pl.CostEstimate(
            flops=2 * 4 * BLK * k * n * BLK,
            bytes_accessed=n * (k + 4 * BLK) * BLK * 2,
            transcendentals=0,
        ),
        compiler_params=pltpu.CompilerParams(vmem_limit_bytes=20 << 20),
    )(*lefts, *groups, *([] if first else [out]))


def place_body(wheres, *refs):
    n = len(wheres)
    parts, (out, sems) = refs[:n], refs[n + 1 :]
    copies = []
    for part, where in zip(parts, wheres):
        for i, (band, dx, dz) in enumerate(where):
            copy = pltpu.make_async_copy(
                part.at[i],
                out.at[band, :, :, pl.ds(column(dx, dz, True), BLK)],
                sems.at[len(copies)],
            )
            copy.start()
            copies.append(copy)
    for copy in copies:
        copy.wait()


def place(out, parts, wheres):
    count = sum(len(w) for w in wheres)
    hbm = pl.BlockSpec(memory_space=pl.ANY)
    return pl.pallas_call(
        functools.partial(place_body, wheres),
        out_shape=jax.ShapeDtypeStruct(out.shape, out.dtype),
        in_specs=[pl.BlockSpec(memory_space=pltpu.VMEM)] * len(parts) + [hbm],
        out_specs=hbm,
        scratch_shapes=[pltpu.SemaphoreType.DMA((count,))],
        input_output_aliases={len(parts): 0},
        cost_estimate=pl.CostEstimate(
            flops=0, bytes_accessed=count * 4 * BLK * BLK * 2, transcendentals=0
        ),
        compiler_params=pltpu.CompilerParams(vmem_limit_bytes=20 << 20),
    )(*parts, out)


def body(spectra, taps):
    return stack_pairs(features_of(spectra, taps), 1.0 / (spectra.shape[1] * BAND_BINS))


def stack_pairs(features, scale):
    out_shape = jax.ShapeDtypeStruct((2, 2, BLK, 64 * BLK), jnp.bfloat16)

    f0, f1 = features[0], features[1]

    zu1, zd1 = move(f1, dz=1), move(f1, dz=-1)
    x2 = move(features, dx=2)
    partner = move(features, dy=2)
    xm, xp = move(features, dx=1), move(features, dx=-1)
    lefts = (left_rows(features), left_rows(partner))

    zu2, zd2 = move(zu1, dz=1), move(zd1, dz=-1)
    zu3, zd3 = move(zu2, dz=1), move(zd2, dz=-1)
    z4 = move(zu3, dz=1)
    near = jnp.stack([zu1, zd1, zu2, zd2])
    near_dz = (-1, 1, -2, 2)
    nm, np_ = move(near, dx=1), move(near, dx=-1)
    nf = move(nm, dx=1)
    far = jnp.stack([zu3, zd3, z4])
    far_dz = (-3, 3, 4)
    fm, fp = move(far, dx=1), move(far, dx=-1)
    ff = move(fp, dx=-1)

    row = jnp.stack([f0, xm[0], xp[0], x2[0]])
    row_dx = (0, -1, 1, 2)
    up1, dn1 = move(row, dz=1), move(row, dz=-1)
    up2, dn2 = move(up1, dz=1), move(dn1, dz=-1)
    up3, dn3 = move(up2, dz=1), move(dn2, dz=-1)
    up4, dn4 = move(up3[:2], dz=1), move(dn3[2:], dz=-1)

    def at_z(g, dz, dxs=row_dx):
        return [(g, i, 0, dx, dz, False, True) for i, dx in enumerate(dxs)]

    def at_x(g, dx, dzs):
        return [(g, i, 1, dx, dz, False, True) for i, dz in enumerate(dzs)]

    work = [
        (
            [row, xm, xp, x2, near],
            at_z(0, 0)[1:]
            + [(g, 1, 1, dx, 0, False, True) for g, dx in zip((1, 2, 3), row_dx[1:])]
            + at_x(4, 0, near_dz),
        ),
        (
            [nm, np_, far, features, partner],
            at_x(0, -1, near_dz)
            + at_x(1, 1, near_dz)
            + at_x(2, 0, far_dz)
            + [(g, b, b, 0, 0, g == 4, False) for b in (1, 0) for g in (3, 4)],
        ),
        ([fm, fp, up1, dn1], at_x(0, -1, far_dz) + at_x(1, 1, far_dz) + at_z(2, -1) + at_z(3, 1)),
        (
            [nf, ff, up2, dn2],
            at_x(0, 2, near_dz) + at_x(1, 2, far_dz) + at_z(2, -2) + at_z(3, 2),
        ),
        ([up3, dn3], at_z(0, -3) + at_z(1, 3)),
        ([up4, dn4], at_z(0, 4, row_dx[:2]) + at_z(1, 4, row_dx[2:])),
    ]
    out = None
    arrived = []
    for groups, items in work:
        out, sent = cross(out, lefts, groups, items, scale, out_shape)
        got = move(sent, dy=2)
        arrived.append((got, [(i[2], i[3], i[4]) for i in items if i[6]]))
    for part in (arrived[:4], arrived[4:5], arrived[5:]):
        out = place(out, [a[0] for a in part], [a[1] for a in part])
    return out


def solution(mesh):
    split = Mesh(mesh.devices.reshape(SIZES), AXES)
    placed = (P(None, None, BAND, CHAN), P())
    return jax.shard_map(
        body, mesh=split, in_specs=placed, out_specs=P(BAND, None, CHAN, None), check_vma=False
    )
```

time: 525 us -> 244 us (0.46)
  the two profiles are of different devices: /device:TPU:8 before, /device:TPU:16 now
where the time goes in v1:
time: 244 us
  waiting for transfers between devices  167 us (68%)
  starting transfers between devices  46.8 us (19%)
  Pallas kernels  24.1 us (10%)
  local copies, waits for them, and re-layouts  5.05 us (2%)
    ppermute x31, waiting for transfers between devices, move(): return lax.ppermute(value, AXES, shifted(**delta))  160 us
    ppermute x31, starting transfers between devices, move(): return lax.ppermute(value, AXES, shifted(**delta))  38.4 us
    pallas_call x6, Pallas kernels, cross(): pl.pallas_call(functools.partial(cross_body, items, scale, len(groups), f...  12.4 us
    pallas_call x4, Pallas kernels, simple_call(): pl.pallas_call(kernel, out_shape=outs, in_specs=[pl.BlockSpec(memory_spac...  8.06 us
  transfers between devices with their start and end apart: 35, of which 19 were waited for; matrix products, arithmetic and copies ran while one was open for 1% of the time, Pallas kernels for 6%

profile of v1, /device:TPU:16, one launch (start us, length us, event | category | flops | bytes accessed | tf_op | source)
XLA Modules:
  0.0 243.6 jit_solution(3405100530135084538)
XLA Ops:
  4.2 3.8 %collective-permute-start.1 = (f32[2,24,8,32]{3,2,1,0:T(8,128)S(1)}, f32[2,24,8,32]{3,2,1,0:T(8,128)S(1)}, u32[]{:S(2)}, u32[]{:S(2)}) collective-permute-start(f32[2,24,8,32]{3,2,1,0:T(8,128)S(1)} %bitcast.27), channel_id=1, source_target_pairs={{4,0},{8,4},{12,8},{16,12},{20,16},{24,20},{28,24},{32,28},{36,32}... | collective-permute-start | bytes 147464 | tf_op jit(solution)/shard_map/ppermute | solution.py:132
  10.1 2.4 collective-permute-done
  13.1 7.3 %shard_map.28 = (f32[2,24,32,128]{3,2,1,0:T(8,128)S(1)}, f32[24,32,128]{2,1,0:T(8,128)S(1)}) custom-call(f32[2,24,32,128]{3,2,1,0:T(8,128)S(1)} %bitcast.16, f32[2,24,32,8]{3,2,1,0:T(8,128)S(1)} %bitcast.17, f32[2,24,32,8]{3,2,1,0:T(8,128)S(1)} %bitcast.18, f32[1536]{0:T(1024)S(1)} %reshape.3.taps_ref), custom_call_target="tpu_custom_call" | custom-call | flops 8282112 | bytes 2070528 | tf_op jit(solution)/shard_map/pallas_call | solution.py:104
  23.0 4.2 %collective-permute-done.3.above_ref = f32[2,32,128]{2,1,0:T(8,128)S(1)} collective-permute-done((f32[2,32,128]{2,1,0:T(8,128)S(1)}, f32[2,32,128]{2,1,0:T(8,128)S(1)}, u32[]{:S(2)}, u32[]{:S(2)}) %collective-permute-start.3) | collective-permute-done | bytes 32800 | tf_op jit(solution)/shard_map/ppermute | solution.py:145
  32.9 6.5 %collective-permute-done.5.refs_3_ = bf16[2,768,128]{2,1,0:T(8,128)(2,1)S(1)} collective-permute-done((bf16[2,768,128]{2,1,0:T(8,128)(2,1)S(1)}, bf16[2,768,128]{2,1,0:T(8,128)(2,1)S(1)}, u32[]{:S(2)}, u32[]{:S(2)}) %collective-permute-start.5) | collective-permute-done | bytes 393248 | tf_op jit(solution)/shard_map/ppermute | solution.py:33
  39.9 8.8 %collective-permute-done.7.refs_5_ = bf16[2,768,128]{2,1,0:T(8,128)(2,1)S(1)} collective-permute-done((bf16[2,768,128]{2,1,0:T(8,128)(2,1)S(1)}, bf16[2,768,128]{2,1,0:T(8,128)(2,1)S(1)}, u32[]{:S(2)}, u32[]{:S(2)}) %collective-permute-start.7) | collective-permute-done | bytes 393248 | tf_op jit(solution)/shard_map/ppermute | solution.py:33
  51.0 4.9 %collective-permute-start.17 = (bf16[768,128]{1,0:T(8,128)(2,1)S(1)}, bf16[768,128]{1,0:T(8,128)(2,1)S(1)}, u32[]{:S(2)}, u32[]{:S(2)}) collective-permute-start(bf16[768,128]{1,0:T(8,128)(2,1)S(1)} %get-tuple-element.35), channel_id=1, source_target_pairs={{0,28},{1,29},{2,30},{3,31},{4,0},{5,1},{6,2},{7,3},{8,4},{9,5},{1... | collective-permute-start | bytes 589832 | tf_op jit(solution)/shard_map/ppermute | solution.py:33
  57.9 19.7 %collective-permute-done.16 = bf16[768,128]{1,0:T(8,128)(2,1)S(1)} collective-permute-done((bf16[768,128]{1,0:T(8,128)(2,1)S(1)}, bf16[768,128]{1,0:T(8,128)(2,1)S(1)}, u32[]{:S(2)}, u32[]{:S(2)}) %collective-permute-start.16) | collective-permute-done | bytes 196640 | tf_op jit(solution)/shard_map/ppermute | solution.py:33
  77.6 3.2 %collective-permute-start.19 = (bf16[768,128]{1,0:T(8,128)(2,1)S(1)}, bf16[768,128]{1,0:T(8,128)(2,1)S(1)}, u32[]{:S(2)}, u32[]{:S(2)}) collective-permute-start(bf16[768,128]{1,0:T(8,128)(2,1)S(1)} %collective-permute-done.17), channel_id=1, source_target_pairs={{0,28},{1,29},{2,30},{3,31},{4,0},{5,1},{6,2},{7,3},{8,4},{9,5},{1... | collective-permute-start | bytes 589832 | tf_op jit(solution)/shard_map/ppermute | solution.py:33
  80.8 5.4 %collective-permute-done.18 = bf16[768,128]{1,0:T(8,128)(2,1)S(1)} collective-permute-done((bf16[768,128]{1,0:T(8,128)(2,1)S(1)}, bf16[768,128]{1,0:T(8,128)(2,1)S(1)}, u32[]{:S(2)}, u32[]{:S(2)}) %collective-permute-start.18) | collective-permute-done | bytes 196640 | tf_op jit(solution)/shard_map/ppermute | solution.py:33
  86.2 3.2 %collective-permute-start.23 = (bf16[768,128]{1,0:T(8,128)(2,1)S(1)}, bf16[768,128]{1,0:T(8,128)(2,1)S(1)}, u32[]{:S(2)}, u32[]{:S(2)}) collective-permute-start(bf16[768,128]{1,0:T(8,128)(2,1)S(1)} %collective-permute-done.19), channel_id=1, source_target_pairs={{0,28},{1,29},{2,30},{3,31},{4,0},{5,1},{6,2},{7,3},{8,4},{9,5},{1... | collective-permute-start | bytes 589832 | tf_op jit(solution)/shard_map/ppermute | solution.py:33
  89.4 4.5 %collective-permute-done.22 = bf16[768,128]{1,0:T(8,128)(2,1)S(1)} collective-permute-done((bf16[768,128]{1,0:T(8,128)(2,1)S(1)}, bf16[768,128]{1,0:T(8,128)(2,1)S(1)}, u32[]{:S(2)}, u32[]{:S(2)}) %collective-permute-start.22) | collective-permute-done | bytes 196640 | tf_op jit(solution)/shard_map/ppermute | solution.py:33
  95.7 7.3 %collective-permute-done.24 = bf16[768,128]{1,0:T(8,128)(2,1)S(1)} collective-permute-done((bf16[768,128]{1,0:T(8,128)(2,1)S(1)}, bf16[768,128]{1,0:T(8,128)(2,1)S(1)}, u32[]{:S(2)}, u32[]{:S(2)}) %collective-permute-start.24) | collective-permute-done | bytes 196640 | tf_op jit(solution)/shard_map/ppermute | solution.py:33
  106.7 11.1 %collective-permute-done.9.refs_4_ = bf16[4,768,128]{2,1,0:T(8,128)(2,1)S(1)} collective-permute-done((bf16[4,768,128]{2,1,0:T(8,128)(2,1)S(1)}, bf16[4,768,128]{2,1,0:T(8,128)(2,1)S(1)}, u32[]{:S(2)}, u32[]{:S(2)}) %collective-permute-start.9) | collective-permute-done | bytes 786464 | tf_op jit(solution)/shard_map/ppermute | solution.py:33
  118.9 4.5 %collective-permute-done.28.refs_3_ = bf16[4,768,128]{2,1,0:T(8,128)(2,1)S(1)} collective-permute-done((bf16[4,768,128]{2,1,0:T(8,128)(2,1)S(1)}, bf16[4,768,128]{2,1,0:T(8,128)(2,1)S(1)}, u32[]{:S(2)}, u32[]{:S(2)}) %collective-permute-start.28) | collective-permute-done | bytes 786464 | tf_op jit(solution)/shard_map/ppermute | solution.py:33
  124.8 8.3 %collective-permute-done.25.refs_3_ = bf16[3,768,128]{2,1,0:T(8,128)(2,1)S(1)} collective-permute-done((bf16[3,768,128]{2,1,0:T(8,128)(2,1)S(1)}, bf16[3,768,128]{2,1,0:T(8,128)(2,1)S(1)}, u32[]{:S(2)}, u32[]{:S(2)}) %collective-permute-start.25) | collective-permute-done | bytes 589856 | tf_op jit(solution)/shard_map/ppermute | solution.py:33
  138.9 10.2 %collective-permute-done.27.refs_2_ = bf16[3,768,128]{2,1,0:T(8,128)(2,1)S(1)} collective-permute-done((bf16[3,768,128]{2,1,0:T(8,128)(2,1)S(1)}, bf16[3,768,128]{2,1,0:T(8,128)(2,1)S(1)}, u32[]{:S(2)}, u32[]{:S(2)}) %collective-permute-start.27) | collective-permute-done | bytes 589856 | tf_op jit(solution)/shard_map/ppermute | solution.py:33
  151.6 2.6 %shard_map.35 = (bf16[2,2,128,8192]{3,2,1,0:T(8,128)(2,1)}, bf16[15,2,128,128]{3,2,1,0:T(8,128)(2,1)S(1)}) custom-call(bf16[2,256,768]{2,1,0:T(8,128)(2,1)S(1)} %shard_map.30.refs_0_, bf16[2,256,768]{2,1,0:T(8,128)(2,1)S(1)} %shard_map.31.refs_1_, bf16[4,768,128]{2,1,0:T(8,128)(2,1)S(1)} %collective-permute-done.21.refs_2_, ...), custom_call_target="tpu_custom_call", output_to_operand_aliasing={{0}: (6, {})} | custom-call | flops 1509949440 | bytes 4915200 | tf_op jit(solution)/shard_map/pallas_call | solution.py:210
  154.3 3.5 %collective-permute-start.33 = (bf16[14,2,128,128]{3,2,1,0:T(8,128)(2,1)S(1)}, bf16[14,2,128,128]{3,2,1,0:T(8,128)(2,1)S(1)}, u32[]{:S(2)}, u32[]{:S(2)}) collective-permute-start(bf16[14,2,128,128]{3,2,1,0:T(8,128)(2,1)S(1)} %get-tuple-element.30), channel_id=1, source_target_pairs={{0,32},{1,33},{2,34},{3,35},{4,36},{5,37},{6,38},{7,39},{8,40},{9,... | collective-permute-start | bytes 2752520 | tf_op jit(solution)/shard_map/ppermute | solution.py:33
  157.9 3.3 %collective-permute-start.15 = (bf16[2,768,128]{2,1,0:T(8,128)(2,1)S(1)}, bf16[2,768,128]{2,1,0:T(8,128)(2,1)S(1)}, u32[]{:S(2)}, u32[]{:S(2)}) collective-permute-start(bf16[2,768,128]{2,1,0:T(8,128)(2,1)S(1)} %slice.49), channel_id=1, source_target_pairs={{0,28},{1,29},{2,30},{3,31},{4,0},{5,1},{6,2},{7,3},{8,4},{9,5},{1... | collective-permute-start | bytes 1179656 | tf_op jit(solution)/shard_map/ppermute | solution.py:33
  161.3 3.4 %collective-permute-start.32 = (bf16[11,2,128,128]{3,2,1,0:T(8,128)(2,1)S(1)}, bf16[11,2,128,128]{3,2,1,0:T(8,128)(2,1)S(1)}, u32[]{:S(2)}, u32[]{:S(2)}) collective-permute-start(bf16[11,2,128,128]{3,2,1,0:T(8,128)(2,1)S(1)} %get-tuple-element.29), channel_id=1, source_target_pairs={{0,32},{1,33},{2,34},{3,35},{4,36},{5,37},{6,38},{7,39},{8,40},{9,... | collective-permute-start | bytes 2162696 | tf_op jit(solution)/shard_map/ppermute | solution.py:33
  167.9 46.3 %collective-permute-done.31.refs_0_ = bf16[10,2,128,128]{3,2,1,0:T(8,128)(2,1)S(1)} collective-permute-done((bf16[10,2,128,128]{3,2,1,0:T(8,128)(2,1)S(1)}, bf16[10,2,128,128]{3,2,1,0:T(8,128)(2,1)S(1)}, u32[]{:S(2)}, u32[]{:S(2)}) %collective-permute-start.31) | collective-permute-done | bytes 655392 | tf_op jit(solution)/shard_map/ppermute | solution.py:33
  214.2 15.4 %collective-permute-done.32.refs_1_ = bf16[11,2,128,128]{3,2,1,0:T(8,128)(2,1)S(1)} collective-permute-done((bf16[11,2,128,128]{3,2,1,0:T(8,128)(2,1)S(1)}, bf16[11,2,128,128]{3,2,1,0:T(8,128)(2,1)S(1)}, u32[]{:S(2)}, u32[]{:S(2)}) %collective-permute-start.32) | collective-permute-done | bytes 720928 | tf_op jit(solution)/shard_map/ppermute | solution.py:33
  231.7 8.1 %collective-permute-done.30.refs_0_ = bf16[8,2,128,128]{3,2,1,0:T(8,128)(2,1)S(1)} collective-permute-done((bf16[8,2,128,128]{3,2,1,0:T(8,128)(2,1)S(1)}, bf16[8,2,128,128]{3,2,1,0:T(8,128)(2,1)S(1)}, u32[]{:S(2)}, u32[]{:S(2)}) %collective-permute-start.30) | collective-permute-done | bytes 524320 | tf_op jit(solution)/shard_map/ppermute | solution.py:33
  (77 shorter events, 45.1 us)
Async XLA Ops:
  27.7 11.6 %collective-permute-start.5 = (bf16[2,768,128]{2,1,0:T(8,128)(2,1)S(1)}, bf16[2,768,128]{2,1,0:T(8,128)(2,1)S(1)}, u32[]{:S(2)}, u32[]{:S(2)}) collective-permute-start(bf16[2,768,128]{2,1,0:T(8,128)(2,1)S(1)} %shard_map.29.feat_ref.refs_5_), channel_id=1, source_target_pairs={{0,64},{1,65},{2,66},{3,67},{4,68},{5,69},{6,70},{7,71},{8,72},{9,... | collective-permute-start | bytes 1179656 | tf_op jit(solution)/shard_map/ppermute | solution.py:33
  29.3 10.6 %collective-permute-start.6 = (bf16[2,768,128]{2,1,0:T(8,128)(2,1)S(1)}, bf16[2,768,128]{2,1,0:T(8,128)(2,1)S(1)}, u32[]{:S(2)}, u32[]{:S(2)}) collective-permute-start(bf16[2,768,128]{2,1,0:T(8,128)(2,1)S(1)} %shard_map.29.feat_ref.refs_5_), channel_id=1, source_target_pairs={{0,192},{1,193},{2,194},{3,195},{4,196},{5,197},{6,198},{7,199},{8... | collective-permute-start | bytes 1179656 | tf_op jit(solution)/shard_map/ppermute | solution.py:33
  31.0 17.7 %collective-permute-start.7 = (bf16[2,768,128]{2,1,0:T(8,128)(2,1)S(1)}, bf16[2,768,128]{2,1,0:T(8,128)(2,1)S(1)}, u32[]{:S(2)}, u32[]{:S(2)}) collective-permute-start(bf16[2,768,128]{2,1,0:T(8,128)(2,1)S(1)} %shard_map.29.feat_ref.refs_5_), channel_id=1, source_target_pairs={{0,128},{1,129},{2,130},{3,131},{4,132},{5,133},{6,134},{7,135},{8... | collective-permute-start | bytes 1179656 | tf_op jit(solution)/shard_map/ppermute | solution.py:33
  48.9 45.1 %collective-permute-start.8 = (bf16[4,768,128]{2,1,0:T(8,128)(2,1)S(1)}, bf16[4,768,128]{2,1,0:T(8,128)(2,1)S(1)}, u32[]{:S(2)}, u32[]{:S(2)}) collective-permute-start(bf16[4,768,128]{2,1,0:T(8,128)(2,1)S(1)} %pad_maximum_fusion.refs_2_), channel_id=1, source_target_pairs={{0,4},{1,5},{2,6},{3,7},{4,8},{5,9},{6,10},{7,11},{8,12},{9,13},{1... | collective-permute-start | bytes 2359304 | tf_op jit(solution)/shard_map/ppermute | solution.py:33
  49.0 28.6 %collective-permute-start.16 = (bf16[768,128]{1,0:T(8,128)(2,1)S(1)}, bf16[768,128]{1,0:T(8,128)(2,1)S(1)}, u32[]{:S(2)}, u32[]{:S(2)}) collective-permute-start(bf16[768,128]{1,0:T(8,128)(2,1)S(1)} %get-tuple-element.35), channel_id=1, source_target_pairs={{0,4},{1,5},{2,6},{3,7},{4,8},{5,9},{6,10},{7,11},{8,12},{9,13},{1... | collective-permute-start | bytes 589832 | tf_op jit(solution)/shard_map/ppermute | solution.py:33
  51.0 26.6 %collective-permute-start.17 = (bf16[768,128]{1,0:T(8,128)(2,1)S(1)}, bf16[768,128]{1,0:T(8,128)(2,1)S(1)}, u32[]{:S(2)}, u32[]{:S(2)}) collective-permute-start(bf16[768,128]{1,0:T(8,128)(2,1)S(1)} %get-tuple-element.35), channel_id=1, source_target_pairs={{0,28},{1,29},{2,30},{3,31},{4,0},{5,1},{6,2},{7,3},{8,4},{9,5},{1... | collective-permute-start | bytes 589832 | tf_op jit(solution)/shard_map/ppermute | solution.py:33
  55.9 47.8 %collective-permute-start.12 = (bf16[4,768,128]{2,1,0:T(8,128)(2,1)S(1)}, bf16[4,768,128]{2,1,0:T(8,128)(2,1)S(1)}, u32[]{:S(2)}, u32[]{:S(2)}) collective-permute-start(bf16[4,768,128]{2,1,0:T(8,128)(2,1)S(1)} %pad_maximum_fusion.refs_2_), channel_id=1, source_target_pairs={{0,28},{1,29},{2,30},{3,31},{4,0},{5,1},{6,2},{7,3},{8,4},{9,5},{1... | collective-permute-start | bytes 2359304 | tf_op jit(solution)/shard_map/ppermute | solution.py:33
  94.0 11.4 %collective-permute-start.4 = (bf16[2,768,128]{2,1,0:T(8,128)(2,1)S(1)}, bf16[2,768,128]{2,1,0:T(8,128)(2,1)S(1)}, u32[]{:S(2)}, u32[]{:S(2)}) collective-permute-start(bf16[2,768,128]{2,1,0:T(8,128)(2,1)S(1)} %shard_map.29.feat_ref.refs_5_), channel_id=1, source_target_pairs={{0,32},{1,33},{2,34},{3,35},{4,36},{5,37},{6,38},{7,39},{8,40},{9,... | collective-permute-start | bytes 1179656 | tf_op jit(solution)/shard_map/ppermute | solution.py:33
  94.0 23.8 %collective-permute-start.9 = (bf16[4,768,128]{2,1,0:T(8,128)(2,1)S(1)}, bf16[4,768,128]{2,1,0:T(8,128)(2,1)S(1)}, u32[]{:S(2)}, u32[]{:S(2)}) collective-permute-start(bf16[4,768,128]{2,1,0:T(8,128)(2,1)S(1)} %collective-permute-done.8.refs_4_), channel_id=1, source_target_pairs={{0,4},{1,5},{2,6},{3,7},{4,8},{5,9},{6,10},{7,11},{8,12},{9,13},{1... | collective-permute-start | bytes 2359304 | tf_op jit(solution)/shard_map/ppermute | solution.py:33
  94.2 23.6 %collective-permute-start.20 = (bf16[4,768,128]{2,1,0:T(8,128)(2,1)S(1)}, bf16[4,768,128]{2,1,0:T(8,128)(2,1)S(1)}, u32[]{:S(2)}, u32[]{:S(2)}) collective-permute-start(bf16[4,768,128]{2,1,0:T(8,128)(2,1)S(1)} %pad_maximum_fusion.1.refs_6_), channel_id=1, source_target_pairs={{0,64},{1,65},{2,66},{3,67},{4,68},{5,69},{6,70},{7,71},{8,72},{9,... | collective-permute-start | bytes 2359304 | tf_op jit(solution)/shard_map/ppermute | solution.py:33
  103.0 20.4 %collective-permute-start.28 = (bf16[4,768,128]{2,1,0:T(8,128)(2,1)S(1)}, bf16[4,768,128]{2,1,0:T(8,128)(2,1)S(1)}, u32[]{:S(2)}, u32[]{:S(2)}) collective-permute-start(bf16[4,768,128]{2,1,0:T(8,128)(2,1)S(1)} %pad_maximum_fusion.1.refs_6_), channel_id=1, source_target_pairs={{0,192},{1,193},{2,194},{3,195},{4,196},{5,197},{6,198},{7,199},{8... | collective-permute-start | bytes 2359304 | tf_op jit(solution)/shard_map/ppermute | solution.py:33
  103.8 30.3 %collective-permute-start.13 = (bf16[4,768,128]{2,1,0:T(8,128)(2,1)S(1)}, bf16[4,768,128]{2,1,0:T(8,128)(2,1)S(1)}, u32[]{:S(2)}, u32[]{:S(2)}) collective-permute-start(bf16[4,768,128]{2,1,0:T(8,128)(2,1)S(1)} %collective-permute-done.12.refs_5_), channel_id=1, source_target_pairs={{0,28},{1,29},{2,30},{3,31},{4,0},{5,1},{6,2},{7,3},{8,4},{9,5},{1... | collective-permute-start | bytes 2359304 | tf_op jit(solution)/shard_map/ppermute | solution.py:33
  105.4 27.7 %collective-permute-start.25 = (bf16[3,768,128]{2,1,0:T(8,128)(2,1)S(1)}, bf16[3,768,128]{2,1,0:T(8,128)(2,1)S(1)}, u32[]{:S(2)}, u32[]{:S(2)}) collective-permute-start(bf16[3,768,128]{2,1,0:T(8,128)(2,1)S(1)} %pad_maximum_fusion.2.refs_4_), channel_id=1, source_target_pairs={{0,192},{1,193},{2,194},{3,195},{4,196},{5,197},{6,198},{7,199},{8... | collective-permute-start | bytes 1769480 | tf_op jit(solution)/shard_map/ppermute | solution.py:33
  117.7 33.7 %collective-permute-start.10 = (bf16[4,768,128]{2,1,0:T(8,128)(2,1)S(1)}, bf16[4,768,128]{2,1,0:T(8,128)(2,1)S(1)}, u32[]{:S(2)}, u32[]{:S(2)}) collective-permute-start(bf16[4,768,128]{2,1,0:T(8,128)(2,1)S(1)} %collective-permute-done.9.refs_4_), channel_id=1, source_target_pairs={{0,4},{1,5},{2,6},{3,7},{4,8},{5,9},{6,10},{7,11},{8,12},{9,13},{1... | collective-permute-start | bytes 2359304 | tf_op jit(solution)/shard_map/ppermute | solution.py:33
  117.8 33.9 %collective-permute-start.21 = (bf16[4,768,128]{2,1,0:T(8,128)(2,1)S(1)}, bf16[4,768,128]{2,1,0:T(8,128)(2,1)S(1)}, u32[]{:S(2)}, u32[]{:S(2)}) collective-permute-start(bf16[4,768,128]{2,1,0:T(8,128)(2,1)S(1)} %collective-permute-done.20.refs_2_), channel_id=1, source_target_pairs={{0,64},{1,65},{2,66},{3,67},{4,68},{5,69},{6,70},{7,71},{8,72},{9,... | collective-permute-start | bytes 2359304 | tf_op jit(solution)/shard_map/ppermute | solution.py:33
  123.4 25.7 %collective-permute-start.27 = (bf16[3,768,128]{2,1,0:T(8,128)(2,1)S(1)}, bf16[3,768,128]{2,1,0:T(8,128)(2,1)S(1)}, u32[]{:S(2)}, u32[]{:S(2)}) collective-permute-start(bf16[3,768,128]{2,1,0:T(8,128)(2,1)S(1)} %pad_maximum_fusion.2.refs_4_), channel_id=1, source_target_pairs={{0,64},{1,65},{2,66},{3,67},{4,68},{5,69},{6,70},{7,71},{8,72},{9,... | collective-permute-start | bytes 1769480 | tf_op jit(solution)/shard_map/ppermute | solution.py:33
  133.1 18.5 %collective-permute-start.26 = (bf16[3,768,128]{2,1,0:T(8,128)(2,1)S(1)}, bf16[3,768,128]{2,1,0:T(8,128)(2,1)S(1)}, u32[]{:S(2)}, u32[]{:S(2)}) collective-permute-start(bf16[3,768,128]{2,1,0:T(8,128)(2,1)S(1)} %collective-permute-done.25.refs_3_), channel_id=1, source_target_pairs={{0,192},{1,193},{2,194},{3,195},{4,196},{5,197},{6,198},{7,199},{8... | collective-permute-start | bytes 1769480 | tf_op jit(solution)/shard_map/ppermute | solution.py:33
  134.1 23.7 %collective-permute-start.14 = (bf16[4,768,128]{2,1,0:T(8,128)(2,1)S(1)}, bf16[4,768,128]{2,1,0:T(8,128)(2,1)S(1)}, u32[]{:S(2)}, u32[]{:S(2)}) collective-permute-start(bf16[4,768,128]{2,1,0:T(8,128)(2,1)S(1)} %collective-permute-done.13.refs_5_), channel_id=1, source_target_pairs={{0,28},{1,29},{2,30},{3,31},{4,0},{5,1},{6,2},{7,3},{8,4},{9,5},{1... | collective-permute-start | bytes 2359304 | tf_op jit(solution)/shard_map/ppermute | solution.py:33
  154.2 75.4 %collective-permute-start.34 = (bf16[15,2,128,128]{3,2,1,0:T(8,128)(2,1)S(1)}, bf16[15,2,128,128]{3,2,1,0:T(8,128)(2,1)S(1)}, u32[]{:S(2)}, u32[]{:S(2)}) collective-permute-start(bf16[15,2,128,128]{3,2,1,0:T(8,128)(2,1)S(1)} %get-tuple-element.31), channel_id=1, source_target_pairs={{0,32},{1,33},{2,34},{3,35},{4,36},{5,37},{6,38},{7,39},{8,40},{9,... | collective-permute-start | bytes 2949128 | tf_op jit(solution)/shard_map/ppermute | solution.py:33
  154.3 75.3 %collective-permute-start.33 = (bf16[14,2,128,128]{3,2,1,0:T(8,128)(2,1)S(1)}, bf16[14,2,128,128]{3,2,1,0:T(8,128)(2,1)S(1)}, u32[]{:S(2)}, u32[]{:S(2)}) collective-permute-start(bf16[14,2,128,128]{3,2,1,0:T(8,128)(2,1)S(1)} %get-tuple-element.30), channel_id=1, source_target_pairs={{0,32},{1,33},{2,34},{3,35},{4,36},{5,37},{6,38},{7,39},{8,40},{9,... | collective-permute-start | bytes 2752520 | tf_op jit(solution)/shard_map/ppermute | solution.py:33
  161.2 53.0 %collective-permute-start.31 = (bf16[10,2,128,128]{3,2,1,0:T(8,128)(2,1)S(1)}, bf16[10,2,128,128]{3,2,1,0:T(8,128)(2,1)S(1)}, u32[]{:S(2)}, u32[]{:S(2)}) collective-permute-start(bf16[10,2,128,128]{3,2,1,0:T(8,128)(2,1)S(1)} %get-tuple-element.28), channel_id=1, source_target_pairs={{0,32},{1,33},{2,34},{3,35},{4,36},{5,37},{6,38},{7,39},{8,40},{9,... | collective-permute-start | bytes 1966088 | tf_op jit(solution)/shard_map/ppermute | solution.py:33
  161.3 68.3 %collective-permute-start.32 = (bf16[11,2,128,128]{3,2,1,0:T(8,128)(2,1)S(1)}, bf16[11,2,128,128]{3,2,1,0:T(8,128)(2,1)S(1)}, u32[]{:S(2)}, u32[]{:S(2)}) collective-permute-start(bf16[11,2,128,128]{3,2,1,0:T(8,128)(2,1)S(1)} %get-tuple-element.29), channel_id=1, source_target_pairs={{0,32},{1,33},{2,34},{3,35},{4,36},{5,37},{6,38},{7,39},{8,40},{9,... | collective-permute-start | bytes 2162696 | tf_op jit(solution)/shard_map/ppermute | solution.py:33
  166.5 73.4 %collective-permute-start.30 = (bf16[8,2,128,128]{3,2,1,0:T(8,128)(2,1)S(1)}, bf16[8,2,128,128]{3,2,1,0:T(8,128)(2,1)S(1)}, u32[]{:S(2)}, u32[]{:S(2)}) collective-permute-start(bf16[8,2,128,128]{3,2,1,0:T(8,128)(2,1)S(1)} %get-tuple-element.27), channel_id=1, source_target_pairs={{0,32},{1,33},{2,34},{3,35},{4,36},{5,37},{6,38},{7,39},{8,40},{9,... | collective-permute-start | bytes 1572872 | tf_op jit(solution)/shard_map/ppermute | solution.py:33
  214.2 28.5 %collective-permute-start.29 = (bf16[4,2,128,128]{3,2,1,0:T(8,128)(2,1)S(1)}, bf16[4,2,128,128]{3,2,1,0:T(8,128)(2,1)S(1)}, u32[]{:S(2)}, u32[]{:S(2)}) collective-permute-start(bf16[4,2,128,128]{3,2,1,0:T(8,128)(2,1)S(1)} %get-tuple-element.26), channel_id=1, source_target_pairs={{0,32},{1,33},{2,34},{3,35},{4,36},{5,37},{6,38},{7,39},{8,40},{9,... | collective-permute-start | bytes 786440 | tf_op jit(solution)/shard_map/ppermute | solution.py:33
  (11 other events, 87.7 us)

commit v2 on v1

--- a/solution.py
+++ b/solution.py
@@ -39,55 +39,77 @@
     return up, [(j, i) for i, j in up]
 
 
-def filter_body(x_ref, before_ref, after_ref, taps_ref, filt_ref, amp_ref):
-    bins, taps = x_ref.shape[1], TAPS
-    start = (lax.axis_index("yl") * 2 + lax.axis_index("core")) * bins
+def filter_body(bins_of, x_ref, before_ref, after_ref, taps_ref, *outs):
+    start = (lax.axis_index("yl") * 2 + lax.axis_index("core")) * x_ref.shape[1]
     lanes = lax.broadcasted_iota(jnp.int32, x_ref.shape[2:], 1)
-
-    def one_bin(f, carry):
+    step = 4
+
+    def along(main, halo, lag):
+        if lag == 0:
+            return main
+        inside = lanes >= lag if lag > 0 else lanes < BLK + lag
+        return pltpu.roll(jnp.where(inside, main, halo), -lag % BLK, 1)
+
+    def one_bin(first, filt_ref, amp_ref, i, carry):
+        f = first + i
         power = None
         for k in range(2):
             x = x_ref[k, f]
-            gap = jnp.zeros((x.shape[0], BLK - taps), jnp.float32)
+            gap = jnp.zeros((x.shape[0], BLK - TAPS), jnp.float32)
             halo = jnp.concatenate([after_ref[k, f], gap, before_ref[k, f]], axis=1)
-            total = jnp.zeros_like(x)
-            for t in range(taps):
-                lag = t - taps // 2
-                if lag == 0:
-                    shifted_x = x
-                else:
-                    inside = lanes >= lag if lag > 0 else lanes < BLK + lag
-                    shifted_x = pltpu.roll(jnp.where(inside, x, halo), -lag % BLK, 1)
-                total = total + taps_ref[(start + f) * taps + t] * shifted_x
-            filt_ref[k, f] = total
+            mains = [along(x, halo, b) for b in range(step)]
+            halos = [along(halo, x, b) for b in range(step)]
+            total = None
+            for lead in range(0, TAPS, step):
+                taps = [taps_ref[(start + f) * TAPS + lead + b] for b in range(step)]
+                main = sum(w * v for w, v in zip(taps[1:], mains[1:])) + taps[0] * mains[0]
+                side = sum(w * v for w, v in zip(taps[1:], halos[1:])) + taps[0] * halos[0]
+                part = along(main, side, lead - TAPS // 2)
+                total = part if total is None else total + part
+            filt_ref[k, i] = total
             power = total * total if power is None else power + total * total
-        amp_ref[f] = jnp.sqrt(power)
+        amp_ref[i] = jnp.sqrt(power)
         return carry
 
-    lax.fori_loop(0, bins, one_bin, 0)
-
-
-def whiten_body(filt_ref, amp_ref, below_ref, above_ref, feat_ref, ext):
-    bins, reach = amp_ref.shape[0], SMOOTH // 2
+    for n, (first, count) in enumerate(bins_of):
+        filt_ref, amp_ref = outs[2 * n : 2 * n + 2]
+        lax.fori_loop(
+            0,
+            count,
+            functools.partial(one_bin, first, filt_ref, amp_ref),
+            0,
+            unroll=min(count, 4),
+        )
+
+
+def whiten_body(*refs):
+    *parts, below_ref, above_ref, feat_ref, ext = refs
+    reach = SMOOTH // 2
     ext[:reach] = below_ref[...]
-    ext[reach : reach + bins] = amp_ref[...]
-    ext[reach + bins :] = above_ref[...]
-    windows = amp_ref.shape[1]
-
-    for band in range(2):
-
-        def one_bin(f, carry):
-            g = band * BAND_BINS + f
-            smoothed = jnp.zeros(amp_ref.shape[1:], jnp.float32)
-            for d in range(SMOOTH):
-                smoothed = smoothed + ext[g + d]
-            under = smoothed / SMOOTH + water_level
-            for k in range(2):
-                row = pl.multiple_of((k * BAND_BINS + f) * windows, windows)
-                feat_ref[band, pl.ds(row, windows)] = (filt_ref[k, g] / under).astype(jnp.bfloat16)
-            return carry
-
-        lax.fori_loop(0, BAND_BINS, one_bin, 0)
+    at = reach
+    for n in range(1, len(parts), 2):
+        ext[at : at + parts[n].shape[0]] = parts[n][...]
+        at += parts[n].shape[0]
+    ext[at:] = above_ref[...]
+    windows = ext.shape[1]
+
+    def one_bin(first, filt_ref, i, carry):
+        f = first + i
+        smoothed = jnp.zeros(ext.shape[1:], jnp.float32)
+        for d in range(SMOOTH):
+            smoothed = smoothed + ext[f + d]
+        under = smoothed / SMOOTH + water_level
+        band = lax.div(f, BAND_BINS)
+        for k in range(2):
+            row = pl.multiple_of((k * BAND_BINS + lax.rem(f, BAND_BINS)) * windows, windows)
+            feat_ref[band, pl.ds(row, windows)] = (filt_ref[k, i] / under).astype(jnp.bfloat16)
+        return carry
+
+    first = 0
+    for n in range(0, len(parts), 2):
+        count = parts[n].shape[1]
+        lax.fori_loop(0, count, functools.partial(one_bin, first, parts[n]), 0, unroll=2)
+        first += count
 
 
 def left_body(feat_ref, left_ref):
@@ -131,23 +153,25 @@
     before = lax.ppermute(last, CHAN, up).swapaxes(2, 3)
     after = lax.ppermute(first, CHAN, down).swapaxes(2, 3)
     f32 = jnp.float32
-    filtered, amplitude = simple_call(
-        filter_body,
-        [
-            jax.ShapeDtypeStruct(turned.shape, f32),
-            jax.ShapeDtypeStruct((bins, windows, chan), f32),
-        ],
-        [turned, before, after, taps.reshape(-1)],
-        smem=(3,),
-    )
+    operands = [turned, before, after, taps.reshape(-1)]
+
+    def filtered(*bins_of):
+        shapes = []
+        for _, count in bins_of:
+            shapes.append(jax.ShapeDtypeStruct((2, count, windows, chan), f32))
+            shapes.append(jax.ShapeDtypeStruct((count, windows, chan), f32))
+        return simple_call(functools.partial(filter_body, bins_of), shapes, operands, smem=(3,))
+
+    low, low_amp, high, high_amp = filtered((0, reach), (bins - reach, reach))
     up, down = neighbours(BAND, False)
-    below = lax.ppermute(amplitude[bins - reach :], BAND, up)
-    above = lax.ppermute(amplitude[:reach], BAND, down)
+    below = lax.ppermute(high_amp, BAND, up)
+    above = lax.ppermute(low_amp, BAND, down)
+    mid, mid_amp = filtered((reach, bins - 2 * reach))
     rows = 2 * windows * BAND_BINS
     return simple_call(
         whiten_body,
         [jax.ShapeDtypeStruct((bins // BAND_BINS, rows, chan), jnp.bfloat16)],
-        [filtered, amplitude, below, above],
+        [low, low_amp, mid, mid_amp, high, high_amp, below, above],
         scratch=[pltpu.VMEM((bins + 2 * reach, windows, chan), f32)],
     )[0]
 
@@ -169,7 +193,9 @@
     at = 0
     for k, pair in pairs_of(items):
         band, both = pair[0][2], any(item[6] for item in pair)
-        right = jnp.concatenate([groups[item[0]][item[1]] for item in pair], axis=1)
+        right = jnp.concatenate(
+            [groups[item[0]][... if item[1] == () else item[1]] for item in pair], axis=1
+        )
         width = len(pair) * BLK
         for side in range(2 if both else 1):
             rows = (own_left, pair_left)[side][band]
@@ -302,24 +328,30 @@
 
     work = [
         (
-            [row, xm, xp, x2, near],
-            at_z(0, 0)[1:]
-            + [(g, 1, 1, dx, 0, False, True) for g, dx in zip((1, 2, 3), row_dx[1:])]
-            + at_x(4, 0, near_dz),
+            [xm, xp, x2, zu1, zd1],
+            [
+                (g, b, b, dx, 0, False, True)
+                for b in (0, 1)
+                for g, dx in zip((0, 1, 2), row_dx[1:])
+            ]
+            + [(3, (), 1, 0, -1, False, True), (4, (), 1, 0, 1, False, True)],
         ),
         (
-            [nm, np_, far, features, partner],
-            at_x(0, -1, near_dz)
-            + at_x(1, 1, near_dz)
-            + at_x(2, 0, far_dz)
-            + [(g, b, b, 0, 0, g == 4, False) for b in (1, 0) for g in (3, 4)],
-        ),
+            [zu2, zd2, far],
+            [(0, (), 1, 0, -2, False, True), (1, (), 1, 0, 2, False, True)] + at_x(2, 0, far_dz),
+        ),
+        ([nm, np_], at_x(0, -1, near_dz) + at_x(1, 1, near_dz)),
         ([fm, fp, up1, dn1], at_x(0, -1, far_dz) + at_x(1, 1, far_dz) + at_z(2, -1) + at_z(3, 1)),
         (
             [nf, ff, up2, dn2],
             at_x(0, 2, near_dz) + at_x(1, 2, far_dz) + at_z(2, -2) + at_z(3, 2),
         ),
-        ([up3, dn3], at_z(0, -3) + at_z(1, 3)),
+        (
+            [up3, dn3, features, partner],
+            at_z(0, -3)
+            + at_z(1, 3)
+            + [(g, b, b, 0, 0, g == 3, False) for b in (0, 1) for g in (2, 3)],
+        ),
         ([up4, dn4], at_z(0, 4, row_dx[:2]) + at_z(1, 4, row_dx[2:])),
     ]
     out = None
@@ -328,7 +360,7 @@
         out, sent = cross(out, lefts, groups, items, scale, out_shape)
         got = move(sent, dy=2)
         arrived.append((got, [(i[2], i[3], i[4]) for i in items if i[6]]))
-    for part in (arrived[:4], arrived[4:5], arrived[5:]):
+    for part in (arrived[:5], arrived[5:6], arrived[6:]):
         out = place(out, [a[0] for a in part], [a[1] for a in part])
     return out
 

time: 244 us -> 235 us (0.963)
  waiting for transfers between devices: 167 us -> 156 us
    ppermute x31 -> x32, waiting for transfers between devices: 160 us -> 153 us  [move(): return lax.ppermute(value, AXES, shifted(**delta))]
    ppermute x2, waiting for transfers between devices: 4.21 us -> 0.01 us  [the longest x1 0.01 us: features_of(): below = lax.ppermute(high_amp, BAND, up)]
    ppermute x31 -> x32, starting transfers between devices: 38.4 us -> 40.2 us  [move(): return lax.ppermute(value, AXES, shifted(**delta))]
    pallas_call x6 -> x7, Pallas kernels: 12.4 us -> 13.1 us  [cross(): pl.pallas_call(functools.partial(cross_body, items, scale, len(groups), f...]
    pallas_call x4 -> x5, Pallas kernels: 8.06 us -> 7.39 us  [simple_call(): pl.pallas_call(kernel, out_shape=outs, in_specs=[pl.BlockSpec(memory_spac...]
  transfers between devices with their start and end apart: 35 -> 36, of which waited for: 19 -> 18; matrix products, arithmetic and copies ran while one was open for 1% -> 1% of each run, Pallas kernels for 6% -> 9%
where the time goes in v2:
time: 235 us; the launch traced here: 234 us
  waiting for transfers between devices  156 us (66%)
  starting transfers between devices  48.5 us (21%)
  Pallas kernels  24.2 us (10%)
  local copies, waits for them, and re-layouts  5.05 us (2%)
    ppermute x32, waiting for transfers between devices, move(): return lax.ppermute(value, AXES, shifted(**delta))  153 us
    ppermute x32, starting transfers between devices, move(): return lax.ppermute(value, AXES, shifted(**delta))  40.2 us
    pallas_call x7, Pallas kernels, cross(): pl.pallas_call(functools.partial(cross_body, items, scale, len(groups), f...  13.1 us
    pallas_call x5, Pallas kernels, simple_call(): pl.pallas_call(kernel, out_shape=outs, in_specs=[pl.BlockSpec(memory_spac...  7.39 us
  transfers between devices with their start and end apart: 36, of which 18 were waited for; matrix products, arithmetic and copies ran while one was open for 1% of the time, Pallas kernels for 9%

profile of v2, /device:TPU:16, one launch (start us, length us, event | category | flops | bytes accessed | tf_op | source)
XLA Modules:
  0.0 234.4 jit_solution(3341812144441369882)
XLA Ops:
  4.2 3.8 %collective-permute-start.1 = (f32[2,24,8,32]{3,2,1,0:T(8,128)S(1)}, f32[2,24,8,32]{3,2,1,0:T(8,128)S(1)}, u32[]{:S(2)}, u32[]{:S(2)}) collective-permute-start(f32[2,24,8,32]{3,2,1,0:T(8,128)S(1)} %bitcast.30), channel_id=1, source_target_pairs={{4,0},{8,4},{12,8},{16,12},{20,16},{24,20},{28,24},{32,28},{36,32}... | collective-permute-start | bytes 147464 | tf_op jit(solution)/shard_map/ppermute | solution.py:154
  17.3 5.3 %shard_map.29 = (f32[2,20,32,128]{3,2,1,0:T(8,128)S(1)}, f32[20,32,128]{2,1,0:T(8,128)S(1)}) custom-call(f32[2,24,32,128]{3,2,1,0:T(8,128)S(1)} %bitcast.17, f32[2,24,32,8]{3,2,1,0:T(8,128)S(1)} %bitcast.19, f32[2,24,32,8]{3,2,1,0:T(8,128)S(1)} %bitcast.21, f32[1536]{0:T(1024)S(1)} %reshape.3.taps_ref), custom_call_target="tpu_custom_call" | custom-call | flops 7495680 | bytes 1873920 | tf_op jit(solution)/shard_map/pallas_call | solution.py:126
  28.0 5.5 %collective-permute-done.5.refs_2_ = bf16[2,768,128]{2,1,0:T(8,128)(2,1)S(1)} collective-permute-done((bf16[2,768,128]{2,1,0:T(8,128)(2,1)S(1)}, bf16[2,768,128]{2,1,0:T(8,128)(2,1)S(1)}, u32[]{:S(2)}, u32[]{:S(2)}) %collective-permute-start.5) | collective-permute-done | bytes 393248 | tf_op jit(solution)/shard_map/ppermute | solution.py:33
  34.1 8.8 %collective-permute-done.7.refs_4_ = bf16[2,768,128]{2,1,0:T(8,128)(2,1)S(1)} collective-permute-done((bf16[2,768,128]{2,1,0:T(8,128)(2,1)S(1)}, bf16[2,768,128]{2,1,0:T(8,128)(2,1)S(1)}, u32[]{:S(2)}, u32[]{:S(2)}) %collective-permute-start.7) | collective-permute-done | bytes 393248 | tf_op jit(solution)/shard_map/ppermute | solution.py:33
  43.9 3.1 %collective-permute-start.16 = (bf16[768,128]{1,0:T(8,128)(2,1)S(1)}, bf16[768,128]{1,0:T(8,128)(2,1)S(1)}, u32[]{:S(2)}, u32[]{:S(2)}) collective-permute-start(bf16[768,128]{1,0:T(8,128)(2,1)S(1)} %get-tuple-element.47), channel_id=1, source_target_pairs={{0,4},{1,5},{2,6},{3,7},{4,8},{5,9},{6,10},{7,11},{8,12},{9,13},{1... | collective-permute-start | bytes 589832 | tf_op jit(solution)/shard_map/ppermute | solution.py:33
  47.0 4.9 %collective-permute-start.17 = (bf16[768,128]{1,0:T(8,128)(2,1)S(1)}, bf16[768,128]{1,0:T(8,128)(2,1)S(1)}, u32[]{:S(2)}, u32[]{:S(2)}) collective-permute-start(bf16[768,128]{1,0:T(8,128)(2,1)S(1)} %get-tuple-element.47), channel_id=1, source_target_pairs={{0,28},{1,29},{2,30},{3,31},{4,0},{5,1},{6,2},{7,3},{8,4},{9,5},{1... | collective-permute-start | bytes 589832 | tf_op jit(solution)/shard_map/ppermute | solution.py:33
  53.9 19.7 %collective-permute-done.16.refs_5_ = bf16[768,128]{1,0:T(8,128)(2,1)S(1)} collective-permute-done((bf16[768,128]{1,0:T(8,128)(2,1)S(1)}, bf16[768,128]{1,0:T(8,128)(2,1)S(1)}, u32[]{:S(2)}, u32[]{:S(2)}) %collective-permute-start.16) | collective-permute-done | bytes 196640 | tf_op jit(solution)/shard_map/ppermute | solution.py:33
  73.6 3.2 %collective-permute-start.19 = (bf16[768,128]{1,0:T(8,128)(2,1)S(1)}, bf16[768,128]{1,0:T(8,128)(2,1)S(1)}, u32[]{:S(2)}, u32[]{:S(2)}) collective-permute-start(bf16[768,128]{1,0:T(8,128)(2,1)S(1)} %collective-permute-done.17.refs_6_), channel_id=1, source_target_pairs={{0,28},{1,29},{2,30},{3,31},{4,0},{5,1},{6,2},{7,3},{8,4},{9,5},{1... | collective-permute-start | bytes 589832 | tf_op jit(solution)/shard_map/ppermute | solution.py:33
  76.8 5.4 %collective-permute-done.18.refs_2_ = bf16[768,128]{1,0:T(8,128)(2,1)S(1)} collective-permute-done((bf16[768,128]{1,0:T(8,128)(2,1)S(1)}, bf16[768,128]{1,0:T(8,128)(2,1)S(1)}, u32[]{:S(2)}, u32[]{:S(2)}) %collective-permute-start.18) | collective-permute-done | bytes 196640 | tf_op jit(solution)/shard_map/ppermute | solution.py:33
  82.2 3.2 %collective-permute-start.23 = (bf16[768,128]{1,0:T(8,128)(2,1)S(1)}, bf16[768,128]{1,0:T(8,128)(2,1)S(1)}, u32[]{:S(2)}, u32[]{:S(2)}) collective-permute-start(bf16[768,128]{1,0:T(8,128)(2,1)S(1)} %collective-permute-done.19.refs_3_), channel_id=1, source_target_pairs={{0,28},{1,29},{2,30},{3,31},{4,0},{5,1},{6,2},{7,3},{8,4},{9,5},{1... | collective-permute-start | bytes 589832 | tf_op jit(solution)/shard_map/ppermute | solution.py:33
  85.4 4.5 %collective-permute-done.22 = bf16[768,128]{1,0:T(8,128)(2,1)S(1)} collective-permute-done((bf16[768,128]{1,0:T(8,128)(2,1)S(1)}, bf16[768,128]{1,0:T(8,128)(2,1)S(1)}, u32[]{:S(2)}, u32[]{:S(2)}) %collective-permute-start.22) | collective-permute-done | bytes 196640 | tf_op jit(solution)/shard_map/ppermute | solution.py:33
  91.7 7.3 %collective-permute-done.24 = bf16[768,128]{1,0:T(8,128)(2,1)S(1)} collective-permute-done((bf16[768,128]{1,0:T(8,128)(2,1)S(1)}, bf16[768,128]{1,0:T(8,128)(2,1)S(1)}, u32[]{:S(2)}, u32[]{:S(2)}) %collective-permute-start.24) | collective-permute-done | bytes 196640 | tf_op jit(solution)/shard_map/ppermute | solution.py:33
  102.7 11.1 %collective-permute-done.9.refs_4_ = bf16[4,768,128]{2,1,0:T(8,128)(2,1)S(1)} collective-permute-done((bf16[4,768,128]{2,1,0:T(8,128)(2,1)S(1)}, bf16[4,768,128]{2,1,0:T(8,128)(2,1)S(1)}, u32[]{:S(2)}, u32[]{:S(2)}) %collective-permute-start.9) | collective-permute-done | bytes 786464 | tf_op jit(solution)/shard_map/ppermute | solution.py:33
  114.9 4.5 %collective-permute-done.28.refs_3_ = bf16[4,768,128]{2,1,0:T(8,128)(2,1)S(1)} collective-permute-done((bf16[4,768,128]{2,1,0:T(8,128)(2,1)S(1)}, bf16[4,768,128]{2,1,0:T(8,128)(2,1)S(1)}, u32[]{:S(2)}, u32[]{:S(2)}) %collective-permute-start.28) | collective-permute-done | bytes 786464 | tf_op jit(solution)/shard_map/ppermute | solution.py:33
  120.8 8.3 %collective-permute-done.25.refs_3_ = bf16[3,768,128]{2,1,0:T(8,128)(2,1)S(1)} collective-permute-done((bf16[3,768,128]{2,1,0:T(8,128)(2,1)S(1)}, bf16[3,768,128]{2,1,0:T(8,128)(2,1)S(1)}, u32[]{:S(2)}, u32[]{:S(2)}) %collective-permute-start.25) | collective-permute-done | bytes 589856 | tf_op jit(solution)/shard_map/ppermute | solution.py:33
  135.4 9.8 %collective-permute-done.27.refs_2_ = bf16[3,768,128]{2,1,0:T(8,128)(2,1)S(1)} collective-permute-done((bf16[3,768,128]{2,1,0:T(8,128)(2,1)S(1)}, bf16[3,768,128]{2,1,0:T(8,128)(2,1)S(1)}, u32[]{:S(2)}, u32[]{:S(2)}) %collective-permute-start.27) | collective-permute-done | bytes 589856 | tf_op jit(solution)/shard_map/ppermute | solution.py:33
  147.8 2.6 %shard_map.37 = (bf16[2,2,128,8192]{3,2,1,0:T(8,128)(2,1)}, bf16[15,2,128,128]{3,2,1,0:T(8,128)(2,1)S(1)}) custom-call(bf16[2,256,768]{2,1,0:T(8,128)(2,1)S(1)} %shard_map.31.refs_0_, bf16[2,256,768]{2,1,0:T(8,128)(2,1)S(1)} %shard_map.32.refs_1_, bf16[4,768,128]{2,1,0:T(8,128)(2,1)S(1)} %collective-permute-done.21.refs_2_, ...), custom_call_target="tpu_custom_call", output_to_operand_aliasing={{0}: (6, {})} | custom-call | flops 1509949440 | bytes 4915200 | tf_op jit(solution)/shard_map/pallas_call | solution.py:236
  150.4 3.5 %collective-permute-start.35 = (bf16[15,2,128,128]{3,2,1,0:T(8,128)(2,1)S(1)}, bf16[15,2,128,128]{3,2,1,0:T(8,128)(2,1)S(1)}, u32[]{:S(2)}, u32[]{:S(2)}) collective-permute-start(bf16[15,2,128,128]{3,2,1,0:T(8,128)(2,1)S(1)} %get-tuple-element.43), channel_id=1, source_target_pairs={{0,32},{1,33},{2,34},{3,35},{4,36},{5,37},{6,38},{7,39},{8,40},{9,... | collective-permute-start | bytes 2949128 | tf_op jit(solution)/shard_map/ppermute | solution.py:33
  154.0 3.3 %collective-permute-start.15 = (bf16[2,768,128]{2,1,0:T(8,128)(2,1)S(1)}, bf16[2,768,128]{2,1,0:T(8,128)(2,1)S(1)}, u32[]{:S(2)}, u32[]{:S(2)}) collective-permute-start(bf16[2,768,128]{2,1,0:T(8,128)(2,1)S(1)} %slice.41), channel_id=1, source_target_pairs={{0,28},{1,29},{2,30},{3,31},{4,0},{5,1},{6,2},{7,3},{8,4},{9,5},{1... | collective-permute-start | bytes 1179656 | tf_op jit(solution)/shard_map/ppermute | solution.py:33
  157.3 4.1 %collective-permute-done.31.refs_0_ = bf16[8,2,128,128]{3,2,1,0:T(8,128)(2,1)S(1)} collective-permute-done((bf16[8,2,128,128]{3,2,1,0:T(8,128)(2,1)S(1)}, bf16[8,2,128,128]{3,2,1,0:T(8,128)(2,1)S(1)}, u32[]{:S(2)}, u32[]{:S(2)}) %collective-permute-start.31) | collective-permute-done | bytes 524320 | tf_op jit(solution)/shard_map/ppermute | solution.py:33
  161.4 3.5 %collective-permute-start.33 = (bf16[8,2,128,128]{3,2,1,0:T(8,128)(2,1)S(1)}, bf16[8,2,128,128]{3,2,1,0:T(8,128)(2,1)S(1)}, u32[]{:S(2)}, u32[]{:S(2)}) collective-permute-start(bf16[8,2,128,128]{3,2,1,0:T(8,128)(2,1)S(1)} %get-tuple-element.41), channel_id=1, source_target_pairs={{0,32},{1,33},{2,34},{3,35},{4,36},{5,37},{6,38},{7,39},{8,40},{9,... | collective-permute-start | bytes 1572872 | tf_op jit(solution)/shard_map/ppermute | solution.py:33
  168.4 40.8 %collective-permute-done.32.refs_1_ = bf16[5,2,128,128]{3,2,1,0:T(8,128)(2,1)S(1)} collective-permute-done((bf16[5,2,128,128]{3,2,1,0:T(8,128)(2,1)S(1)}, bf16[5,2,128,128]{3,2,1,0:T(8,128)(2,1)S(1)}, u32[]{:S(2)}, u32[]{:S(2)}) %collective-permute-start.32) | collective-permute-done | bytes 327712 | tf_op jit(solution)/shard_map/ppermute | solution.py:33
  209.2 11.2 %collective-permute-done.33.refs_2_ = bf16[8,2,128,128]{3,2,1,0:T(8,128)(2,1)S(1)} collective-permute-done((bf16[8,2,128,128]{3,2,1,0:T(8,128)(2,1)S(1)}, bf16[8,2,128,128]{3,2,1,0:T(8,128)(2,1)S(1)}, u32[]{:S(2)}, u32[]{:S(2)}) %collective-permute-start.33) | collective-permute-done | bytes 524320 | tf_op jit(solution)/shard_map/ppermute | solution.py:33
  222.6 8.2 %collective-permute-done.30.refs_0_ = bf16[8,2,128,128]{3,2,1,0:T(8,128)(2,1)S(1)} collective-permute-done((bf16[8,2,128,128]{3,2,1,0:T(8,128)(2,1)S(1)}, bf16[8,2,128,128]{3,2,1,0:T(8,128)(2,1)S(1)}, u32[]{:S(2)}, u32[]{:S(2)}) %collective-permute-start.30) | collective-permute-done | bytes 524320 | tf_op jit(solution)/shard_map/ppermute | solution.py:33
  (80 shorter events, 48.2 us)
Async XLA Ops:
  26.2 16.8 %collective-permute-start.7 = (bf16[2,768,128]{2,1,0:T(8,128)(2,1)S(1)}, bf16[2,768,128]{2,1,0:T(8,128)(2,1)S(1)}, u32[]{:S(2)}, u32[]{:S(2)}) collective-permute-start(bf16[2,768,128]{2,1,0:T(8,128)(2,1)S(1)} %shard_map.30.feat_ref.refs_4_), channel_id=1, source_target_pairs={{0,128},{1,129},{2,130},{3,131},{4,132},{5,133},{6,134},{7,135},{8... | collective-permute-start | bytes 1179656 | tf_op jit(solution)/shard_map/ppermute | solution.py:33
  43.1 46.9 %collective-permute-start.8 = (bf16[4,768,128]{2,1,0:T(8,128)(2,1)S(1)}, bf16[4,768,128]{2,1,0:T(8,128)(2,1)S(1)}, u32[]{:S(2)}, u32[]{:S(2)}) collective-permute-start(bf16[4,768,128]{2,1,0:T(8,128)(2,1)S(1)} %pad_maximum_fusion), channel_id=1, source_target_pairs={{0,4},{1,5},{2,6},{3,7},{4,8},{5,9},{6,10},{7,11},{8,12},{9,13},{1... | collective-permute-start | bytes 2359304 | tf_op jit(solution)/shard_map/ppermute | solution.py:33
  43.9 29.7 %collective-permute-start.16 = (bf16[768,128]{1,0:T(8,128)(2,1)S(1)}, bf16[768,128]{1,0:T(8,128)(2,1)S(1)}, u32[]{:S(2)}, u32[]{:S(2)}) collective-permute-start(bf16[768,128]{1,0:T(8,128)(2,1)S(1)} %get-tuple-element.47), channel_id=1, source_target_pairs={{0,4},{1,5},{2,6},{3,7},{4,8},{5,9},{6,10},{7,11},{8,12},{9,13},{1... | collective-permute-start | bytes 589832 | tf_op jit(solution)/shard_map/ppermute | solution.py:33
  47.0 26.5 %collective-permute-start.17 = (bf16[768,128]{1,0:T(8,128)(2,1)S(1)}, bf16[768,128]{1,0:T(8,128)(2,1)S(1)}, u32[]{:S(2)}, u32[]{:S(2)}) collective-permute-start(bf16[768,128]{1,0:T(8,128)(2,1)S(1)} %get-tuple-element.47), channel_id=1, source_target_pairs={{0,28},{1,29},{2,30},{3,31},{4,0},{5,1},{6,2},{7,3},{8,4},{9,5},{1... | collective-permute-start | bytes 589832 | tf_op jit(solution)/shard_map/ppermute | solution.py:33
  51.9 47.8 %collective-permute-start.12 = (bf16[4,768,128]{2,1,0:T(8,128)(2,1)S(1)}, bf16[4,768,128]{2,1,0:T(8,128)(2,1)S(1)}, u32[]{:S(2)}, u32[]{:S(2)}) collective-permute-start(bf16[4,768,128]{2,1,0:T(8,128)(2,1)S(1)} %pad_maximum_fusion), channel_id=1, source_target_pairs={{0,28},{1,29},{2,30},{3,31},{4,0},{5,1},{6,2},{7,3},{8,4},{9,5},{1... | collective-permute-start | bytes 2359304 | tf_op jit(solution)/shard_map/ppermute | solution.py:33
  90.0 23.8 %collective-permute-start.9 = (bf16[4,768,128]{2,1,0:T(8,128)(2,1)S(1)}, bf16[4,768,128]{2,1,0:T(8,128)(2,1)S(1)}, u32[]{:S(2)}, u32[]{:S(2)}) collective-permute-start(bf16[4,768,128]{2,1,0:T(8,128)(2,1)S(1)} %collective-permute-done.8.refs_4_), channel_id=1, source_target_pairs={{0,4},{1,5},{2,6},{3,7},{4,8},{5,9},{6,10},{7,11},{8,12},{9,13},{1... | collective-permute-start | bytes 2359304 | tf_op jit(solution)/shard_map/ppermute | solution.py:33
  90.2 23.6 %collective-permute-start.20 = (bf16[4,768,128]{2,1,0:T(8,128)(2,1)S(1)}, bf16[4,768,128]{2,1,0:T(8,128)(2,1)S(1)}, u32[]{:S(2)}, u32[]{:S(2)}) collective-permute-start(bf16[4,768,128]{2,1,0:T(8,128)(2,1)S(1)} %pad_maximum_fusion.1), channel_id=1, source_target_pairs={{0,64},{1,65},{2,66},{3,67},{4,68},{5,69},{6,70},{7,71},{8,72},{9,... | collective-permute-start | bytes 2359304 | tf_op jit(solution)/shard_map/ppermute | solution.py:33
  99.0 20.4 %collective-permute-start.28 = (bf16[4,768,128]{2,1,0:T(8,128)(2,1)S(1)}, bf16[4,768,128]{2,1,0:T(8,128)(2,1)S(1)}, u32[]{:S(2)}, u32[]{:S(2)}) collective-permute-start(bf16[4,768,128]{2,1,0:T(8,128)(2,1)S(1)} %pad_maximum_fusion.1), channel_id=1, source_target_pairs={{0,192},{1,193},{2,194},{3,195},{4,196},{5,197},{6,198},{7,199},{8... | collective-permute-start | bytes 2359304 | tf_op jit(solution)/shard_map/ppermute | solution.py:33
  99.8 30.3 %collective-permute-start.13 = (bf16[4,768,128]{2,1,0:T(8,128)(2,1)S(1)}, bf16[4,768,128]{2,1,0:T(8,128)(2,1)S(1)}, u32[]{:S(2)}, u32[]{:S(2)}) collective-permute-start(bf16[4,768,128]{2,1,0:T(8,128)(2,1)S(1)} %collective-permute-done.12.refs_5_), channel_id=1, source_target_pairs={{0,28},{1,29},{2,30},{3,31},{4,0},{5,1},{6,2},{7,3},{8,4},{9,5},{1... | collective-permute-start | bytes 2359304 | tf_op jit(solution)/shard_map/ppermute | solution.py:33
  101.4 27.7 %collective-permute-start.25 = (bf16[3,768,128]{2,1,0:T(8,128)(2,1)S(1)}, bf16[3,768,128]{2,1,0:T(8,128)(2,1)S(1)}, u32[]{:S(2)}, u32[]{:S(2)}) collective-permute-start(bf16[3,768,128]{2,1,0:T(8,128)(2,1)S(1)} %pad_maximum_fusion.2.refs_4_), channel_id=1, source_target_pairs={{0,192},{1,193},{2,194},{3,195},{4,196},{5,197},{6,198},{7,199},{8... | collective-permute-start | bytes 1769480 | tf_op jit(solution)/shard_map/ppermute | solution.py:33
  113.8 33.8 %collective-permute-start.10 = (bf16[4,768,128]{2,1,0:T(8,128)(2,1)S(1)}, bf16[4,768,128]{2,1,0:T(8,128)(2,1)S(1)}, u32[]{:S(2)}, u32[]{:S(2)}) collective-permute-start(bf16[4,768,128]{2,1,0:T(8,128)(2,1)S(1)} %collective-permute-done.9.refs_4_), channel_id=1, source_target_pairs={{0,4},{1,5},{2,6},{3,7},{4,8},{5,9},{6,10},{7,11},{8,12},{9,13},{1... | collective-permute-start | bytes 2359304 | tf_op jit(solution)/shard_map/ppermute | solution.py:33
  113.8 34.0 %collective-permute-start.21 = (bf16[4,768,128]{2,1,0:T(8,128)(2,1)S(1)}, bf16[4,768,128]{2,1,0:T(8,128)(2,1)S(1)}, u32[]{:S(2)}, u32[]{:S(2)}) collective-permute-start(bf16[4,768,128]{2,1,0:T(8,128)(2,1)S(1)} %collective-permute-done.20.refs_2_), channel_id=1, source_target_pairs={{0,64},{1,65},{2,66},{3,67},{4,68},{5,69},{6,70},{7,71},{8,72},{9,... | collective-permute-start | bytes 2359304 | tf_op jit(solution)/shard_map/ppermute | solution.py:33
  119.4 25.8 %collective-permute-start.27 = (bf16[3,768,128]{2,1,0:T(8,128)(2,1)S(1)}, bf16[3,768,128]{2,1,0:T(8,128)(2,1)S(1)}, u32[]{:S(2)}, u32[]{:S(2)}) collective-permute-start(bf16[3,768,128]{2,1,0:T(8,128)(2,1)S(1)} %pad_maximum_fusion.2.refs_4_), channel_id=1, source_target_pairs={{0,64},{1,65},{2,66},{3,67},{4,68},{5,69},{6,70},{7,71},{8,72},{9,... | collective-permute-start | bytes 1769480 | tf_op jit(solution)/shard_map/ppermute | solution.py:33
  129.2 18.6 %collective-permute-start.26 = (bf16[3,768,128]{2,1,0:T(8,128)(2,1)S(1)}, bf16[3,768,128]{2,1,0:T(8,128)(2,1)S(1)}, u32[]{:S(2)}, u32[]{:S(2)}) collective-permute-start(bf16[3,768,128]{2,1,0:T(8,128)(2,1)S(1)} %collective-permute-done.25.refs_3_), channel_id=1, source_target_pairs={{0,192},{1,193},{2,194},{3,195},{4,196},{5,197},{6,198},{7,199},{8... | collective-permute-start | bytes 1769480 | tf_op jit(solution)/shard_map/ppermute | solution.py:33
  130.1 23.9 %collective-permute-start.14 = (bf16[4,768,128]{2,1,0:T(8,128)(2,1)S(1)}, bf16[4,768,128]{2,1,0:T(8,128)(2,1)S(1)}, u32[]{:S(2)}, u32[]{:S(2)}) collective-permute-start(bf16[4,768,128]{2,1,0:T(8,128)(2,1)S(1)} %collective-permute-done.13.refs_5_), channel_id=1, source_target_pairs={{0,28},{1,29},{2,30},{3,31},{4,0},{5,1},{6,2},{7,3},{8,4},{9,5},{1... | collective-permute-start | bytes 2359304 | tf_op jit(solution)/shard_map/ppermute | solution.py:33
  145.1 16.3 %collective-permute-start.31 = (bf16[8,2,128,128]{3,2,1,0:T(8,128)(2,1)S(1)}, bf16[8,2,128,128]{3,2,1,0:T(8,128)(2,1)S(1)}, u32[]{:S(2)}, u32[]{:S(2)}) collective-permute-start(bf16[8,2,128,128]{3,2,1,0:T(8,128)(2,1)S(1)} %get-tuple-element.39), channel_id=1, source_target_pairs={{0,32},{1,33},{2,34},{3,35},{4,36},{5,37},{6,38},{7,39},{8,40},{9,... | collective-permute-start | bytes 1572872 | tf_op jit(solution)/shard_map/ppermute | solution.py:33
  147.7 13.8 %collective-permute-start.11 = (bf16[2,768,128]{2,1,0:T(8,128)(2,1)S(1)}, bf16[2,768,128]{2,1,0:T(8,128)(2,1)S(1)}, u32[]{:S(2)}, u32[]{:S(2)}) collective-permute-start(bf16[2,768,128]{2,1,0:T(8,128)(2,1)S(1)} %slice.40), channel_id=1, source_target_pairs={{0,4},{1,5},{2,6},{3,7},{4,8},{5,9},{6,10},{7,11},{8,12},{9,13},{1... | collective-permute-start | bytes 1179656 | tf_op jit(solution)/shard_map/ppermute | solution.py:33
  150.4 70.1 %collective-permute-start.35 = (bf16[15,2,128,128]{3,2,1,0:T(8,128)(2,1)S(1)}, bf16[15,2,128,128]{3,2,1,0:T(8,128)(2,1)S(1)}, u32[]{:S(2)}, u32[]{:S(2)}) collective-permute-start(bf16[15,2,128,128]{3,2,1,0:T(8,128)(2,1)S(1)} %get-tuple-element.43), channel_id=1, source_target_pairs={{0,32},{1,33},{2,34},{3,35},{4,36},{5,37},{6,38},{7,39},{8,40},{9,... | collective-permute-start | bytes 2949128 | tf_op jit(solution)/shard_map/ppermute | solution.py:33
  153.9 66.5 %collective-permute-start.34 = (bf16[14,2,128,128]{3,2,1,0:T(8,128)(2,1)S(1)}, bf16[14,2,128,128]{3,2,1,0:T(8,128)(2,1)S(1)}, u32[]{:S(2)}, u32[]{:S(2)}) collective-permute-start(bf16[14,2,128,128]{3,2,1,0:T(8,128)(2,1)S(1)} %get-tuple-element.42), channel_id=1, source_target_pairs={{0,32},{1,33},{2,34},{3,35},{4,36},{5,37},{6,38},{7,39},{8,40},{9,... | collective-permute-start | bytes 2752520 | tf_op jit(solution)/shard_map/ppermute | solution.py:33
  154.0 12.9 %collective-permute-start.15 = (bf16[2,768,128]{2,1,0:T(8,128)(2,1)S(1)}, bf16[2,768,128]{2,1,0:T(8,128)(2,1)S(1)}, u32[]{:S(2)}, u32[]{:S(2)}) collective-permute-start(bf16[2,768,128]{2,1,0:T(8,128)(2,1)S(1)} %slice.41), channel_id=1, source_target_pairs={{0,28},{1,29},{2,30},{3,31},{4,0},{5,1},{6,2},{7,3},{8,4},{9,5},{1... | collective-permute-start | bytes 1179656 | tf_op jit(solution)/shard_map/ppermute | solution.py:33
  161.4 47.8 %collective-permute-start.32 = (bf16[5,2,128,128]{3,2,1,0:T(8,128)(2,1)S(1)}, bf16[5,2,128,128]{3,2,1,0:T(8,128)(2,1)S(1)}, u32[]{:S(2)}, u32[]{:S(2)}) collective-permute-start(bf16[5,2,128,128]{3,2,1,0:T(8,128)(2,1)S(1)} %get-tuple-element.40), channel_id=1, source_target_pairs={{0,32},{1,33},{2,34},{3,35},{4,36},{5,37},{6,38},{7,39},{8,40},{9,... | collective-permute-start | bytes 983048 | tf_op jit(solution)/shard_map/ppermute | solution.py:33
  161.4 59.0 %collective-permute-start.33 = (bf16[8,2,128,128]{3,2,1,0:T(8,128)(2,1)S(1)}, bf16[8,2,128,128]{3,2,1,0:T(8,128)(2,1)S(1)}, u32[]{:S(2)}, u32[]{:S(2)}) collective-permute-start(bf16[8,2,128,128]{3,2,1,0:T(8,128)(2,1)S(1)} %get-tuple-element.41), channel_id=1, source_target_pairs={{0,32},{1,33},{2,34},{3,35},{4,36},{5,37},{6,38},{7,39},{8,40},{9,... | collective-permute-start | bytes 1572872 | tf_op jit(solution)/shard_map/ppermute | solution.py:33
  167.0 63.7 %collective-permute-start.30 = (bf16[8,2,128,128]{3,2,1,0:T(8,128)(2,1)S(1)}, bf16[8,2,128,128]{3,2,1,0:T(8,128)(2,1)S(1)}, u32[]{:S(2)}, u32[]{:S(2)}) collective-permute-start(bf16[8,2,128,128]{3,2,1,0:T(8,128)(2,1)S(1)} %get-tuple-element.38), channel_id=1, source_target_pairs={{0,32},{1,33},{2,34},{3,35},{4,36},{5,37},{6,38},{7,39},{8,40},{9,... | collective-permute-start | bytes 1572872 | tf_op jit(solution)/shard_map/ppermute | solution.py:33
  209.2 24.3 %collective-permute-start.29 = (bf16[4,2,128,128]{3,2,1,0:T(8,128)(2,1)S(1)}, bf16[4,2,128,128]{3,2,1,0:T(8,128)(2,1)S(1)}, u32[]{:S(2)}, u32[]{:S(2)}) collective-permute-start(bf16[4,2,128,128]{3,2,1,0:T(8,128)(2,1)S(1)} %get-tuple-element.37), channel_id=1, source_target_pairs={{0,32},{1,33},{2,34},{3,35},{4,36},{5,37},{6,38},{7,39},{8,40},{9,... | collective-permute-start | bytes 786440 | tf_op jit(solution)/shard_map/ppermute | solution.py:33
  (12 other events, 107.6 us)

commit v3 on v2

--- a/solution.py
+++ b/solution.py
@@ -39,10 +39,30 @@
     return up, [(j, i) for i, j in up]
 
 
+LANE_GROUPS = BLK // (TAPS // 2)
+
+
+def pack_body(x_ref, first_ref, last_ref):
+    edge = TAPS // 2
+    rows = x_ref.shape[0] * x_ref.shape[2]
+    place = lax.broadcasted_iota(jnp.int32, (rows, BLK), 1) // edge
+    for g in range(first_ref.shape[1]):
+        ends = [jnp.zeros((rows, BLK), jnp.float32) for _ in range(2)]
+        for j in range(min(LANE_GROUPS, x_ref.shape[1] - g * LANE_GROUPS)):
+            x = x_ref[:, g * LANE_GROUPS + j].reshape(rows, BLK)
+            for n, lead in enumerate((0, BLK - edge)):
+                shift = (j * edge - lead) % BLK
+                ends[n] = jnp.where(place == j, pltpu.roll(x, shift, 1) if shift else x, ends[n])
+        first_ref[:, g] = ends[0].reshape(x_ref.shape[0], x_ref.shape[2], BLK)
+        last_ref[:, g] = ends[1].reshape(x_ref.shape[0], x_ref.shape[2], BLK)
+
+
 def filter_body(bins_of, x_ref, before_ref, after_ref, taps_ref, *outs):
     start = (lax.axis_index("yl") * 2 + lax.axis_index("core")) * x_ref.shape[1]
-    lanes = lax.broadcasted_iota(jnp.int32, x_ref.shape[2:], 1)
-    step = 4
+    parts, windows = x_ref.shape[0], x_ref.shape[2]
+    rows = parts * windows
+    lanes = lax.broadcasted_iota(jnp.int32, (rows, BLK), 1)
+    step, edge = 4, TAPS // 2
 
     def along(main, halo, lag):
         if lag == 0:
@@ -52,23 +72,24 @@
 
     def one_bin(first, filt_ref, amp_ref, i, carry):
         f = first + i
-        power = None
-        for k in range(2):
-            x = x_ref[k, f]
-            gap = jnp.zeros((x.shape[0], BLK - TAPS), jnp.float32)
-            halo = jnp.concatenate([after_ref[k, f], gap, before_ref[k, f]], axis=1)
-            mains = [along(x, halo, b) for b in range(step)]
-            halos = [along(halo, x, b) for b in range(step)]
-            total = None
-            for lead in range(0, TAPS, step):
-                taps = [taps_ref[(start + f) * TAPS + lead + b] for b in range(step)]
-                main = sum(w * v for w, v in zip(taps[1:], mains[1:])) + taps[0] * mains[0]
-                side = sum(w * v for w, v in zip(taps[1:], halos[1:])) + taps[0] * halos[0]
-                part = along(main, side, lead - TAPS // 2)
-                total = part if total is None else total + part
-            filt_ref[k, i] = total
-            power = total * total if power is None else power + total * total
-        amp_ref[i] = jnp.sqrt(power)
+        x = x_ref[:, f].reshape(rows, BLK)
+        g, lead = lax.div(f, LANE_GROUPS), lax.rem(f, LANE_GROUPS) * edge
+        after = pltpu.roll(after_ref[:, g].reshape(rows, BLK), lax.rem(BLK - lead, BLK), 1)
+        before = pltpu.roll(before_ref[:, g].reshape(rows, BLK), BLK - edge - lead, 1)
+        halo = jnp.where(lanes < edge, after, before)
+        mains = [along(x, halo, b) for b in range(step)]
+        halos = [along(halo, x, b) for b in range(step)]
+        total = None
+        for lead in range(0, TAPS, step):
+            taps = [taps_ref[(start + f) * TAPS + lead + b] for b in range(step)]
+            main, side = taps[0] * mains[0], taps[0] * halos[0]
+            for b in range(1, step):
+                main, side = main + taps[b] * mains[b], side + taps[b] * halos[b]
+            part = along(main, side, lead - edge)
+            total = part if total is None else total + part
+        total = total.reshape(parts, windows, BLK)
+        filt_ref[:, i] = total
+        amp_ref[i] = jnp.sqrt(total[0] * total[0] + total[1] * total[1])
         return carry
 
     for n, (first, count) in enumerate(bins_of):
@@ -144,14 +165,14 @@
 
 
 def features_of(spectra, taps):
-    edge, reach = TAPS // 2, SMOOTH // 2
+    reach = SMOOTH // 2
     turned = spectra.transpose(0, 2, 1, 3)
-    bins, windows, chan = turned.shape[1:]
+    parts, bins, windows, chan = turned.shape
+    ends = jax.ShapeDtypeStruct((parts, pl.cdiv(bins, LANE_GROUPS), windows, chan), jnp.float32)
+    first, last = simple_call(pack_body, [ends, ends], [turned])
     up, down = neighbours(CHAN, True)
-    last = spectra[..., chan - edge :].transpose(0, 2, 3, 1)
-    first = spectra[..., :edge].transpose(0, 2, 3, 1)
-    before = lax.ppermute(last, CHAN, up).swapaxes(2, 3)
-    after = lax.ppermute(first, CHAN, down).swapaxes(2, 3)
+    before = lax.ppermute(last, CHAN, up)
+    after = lax.ppermute(first, CHAN, down)
     f32 = jnp.float32
     operands = [turned, before, after, taps.reshape(-1)]
 

time: 235 us -> 231 us (0.983)
  local copies, waits for them, and re-layouts: 5.05 us -> 2.27 us
    pallas_call x5 -> x6, Pallas kernels: 7.39 us -> 7.1 us  [simple_call(): pl.pallas_call(kernel, out_shape=outs, in_specs=[pl.BlockSpec(memory_spac...]
  transfers between devices with their start and end apart: 36 -> 36, of which waited for: 18 -> 18; matrix products, arithmetic and copies ran while one was open for 1% -> 0% of each run, Pallas kernels for 9% -> 9%
where the time goes in v3:
time: 231 us
  waiting for transfers between devices  155 us (67%)
  starting transfers between devices  49 us (21%)
  Pallas kernels  23.9 us (10%)
    ppermute x32, waiting for transfers between devices, move(): return lax.ppermute(value, AXES, shifted(**delta))  153 us
    ppermute x32, starting transfers between devices, move(): return lax.ppermute(value, AXES, shifted(**delta))  40.6 us
    pallas_call x7, Pallas kernels, cross(): pl.pallas_call(functools.partial(cross_body, items, scale, len(groups), f...  13.1 us
    pallas_call x6, Pallas kernels, simple_call(): pl.pallas_call(kernel, out_shape=outs, in_specs=[pl.BlockSpec(memory_spac...  7.1 us
  transfers between devices with their start and end apart: 36, of which 18 were waited for; matrix products, arithmetic and copies ran while one was open for 0% of the time, Pallas kernels for 9%

profile of v3, /device:TPU:16, one launch (start us, length us, event | category | flops | bytes accessed | tf_op | source)
XLA Modules:
  0.0 230.6 jit_solution(4212964286386045748)
XLA Ops:
  3.7 3.8 %collective-permute-start.1 = (f32[2,2,32,128]{3,2,1,0:T(8,128)S(1)}, f32[2,2,32,128]{3,2,1,0:T(8,128)S(1)}, u32[]{:S(2)}, u32[]{:S(2)}) collective-permute-start(f32[2,2,32,128]{3,2,1,0:T(8,128)S(1)} %get-tuple-element.28), channel_id=1, source_target_pairs={{4,0},{8,4},{12,8},{16,12},{20,16},{24,20},{28,24},{32,28},{36,32}... | collective-permute-start | bytes 196616 | tf_op jit(solution)/shard_map/ppermute | solution.py:175
  13.7 4.7 %shard_map.30 = (f32[2,20,32,128]{3,2,1,0:T(8,128)S(1)}, f32[20,32,128]{2,1,0:T(8,128)S(1)}) custom-call(f32[2,24,32,128]{3,2,1,0:T(8,128)S(1)} %bitcast.14, f32[2,2,32,128]{3,2,1,0:T(8,128)S(1)} %collective-permute-done.before_ref, f32[2,2,32,128]{3,2,1,0:T(8,128)S(1)} %collective-permute-done.1.after_ref, f32[1536]{0:T(1024)S(1)} %reshape.3.taps_ref), custom_call_target="tpu_custom_call" | custom-call | flops 7626752 | bytes 1906688 | tf_op jit(solution)/shard_map/pallas_call | solution.py:147
  23.9 5.6 %collective-permute-done.5.refs_2_ = bf16[2,768,128]{2,1,0:T(8,128)(2,1)S(1)} collective-permute-done((bf16[2,768,128]{2,1,0:T(8,128)(2,1)S(1)}, bf16[2,768,128]{2,1,0:T(8,128)(2,1)S(1)}, u32[]{:S(2)}, u32[]{:S(2)}) %collective-permute-start.5) | collective-permute-done | bytes 393248 | tf_op jit(solution)/shard_map/ppermute | solution.py:33
  30.0 8.8 %collective-permute-done.7.refs_4_ = bf16[2,768,128]{2,1,0:T(8,128)(2,1)S(1)} collective-permute-done((bf16[2,768,128]{2,1,0:T(8,128)(2,1)S(1)}, bf16[2,768,128]{2,1,0:T(8,128)(2,1)S(1)}, u32[]{:S(2)}, u32[]{:S(2)}) %collective-permute-start.7) | collective-permute-done | bytes 393248 | tf_op jit(solution)/shard_map/ppermute | solution.py:33
  40.1 3.0 %collective-permute-start.16 = (bf16[768,128]{1,0:T(8,128)(2,1)S(1)}, bf16[768,128]{1,0:T(8,128)(2,1)S(1)}, u32[]{:S(2)}, u32[]{:S(2)}) collective-permute-start(bf16[768,128]{1,0:T(8,128)(2,1)S(1)} %get-tuple-element.49), channel_id=1, source_target_pairs={{0,4},{1,5},{2,6},{3,7},{4,8},{5,9},{6,10},{7,11},{8,12},{9,13},{1... | collective-permute-start | bytes 589832 | tf_op jit(solution)/shard_map/ppermute | solution.py:33
  43.2 5.0 %collective-permute-start.17 = (bf16[768,128]{1,0:T(8,128)(2,1)S(1)}, bf16[768,128]{1,0:T(8,128)(2,1)S(1)}, u32[]{:S(2)}, u32[]{:S(2)}) collective-permute-start(bf16[768,128]{1,0:T(8,128)(2,1)S(1)} %get-tuple-element.49), channel_id=1, source_target_pairs={{0,28},{1,29},{2,30},{3,31},{4,0},{5,1},{6,2},{7,3},{8,4},{9,5},{1... | collective-permute-start | bytes 589832 | tf_op jit(solution)/shard_map/ppermute | solution.py:33
  50.1 19.7 %collective-permute-done.16.refs_5_ = bf16[768,128]{1,0:T(8,128)(2,1)S(1)} collective-permute-done((bf16[768,128]{1,0:T(8,128)(2,1)S(1)}, bf16[768,128]{1,0:T(8,128)(2,1)S(1)}, u32[]{:S(2)}, u32[]{:S(2)}) %collective-permute-start.16) | collective-permute-done | bytes 196640 | tf_op jit(solution)/shard_map/ppermute | solution.py:33
  69.8 3.2 %collective-permute-start.19 = (bf16[768,128]{1,0:T(8,128)(2,1)S(1)}, bf16[768,128]{1,0:T(8,128)(2,1)S(1)}, u32[]{:S(2)}, u32[]{:S(2)}) collective-permute-start(bf16[768,128]{1,0:T(8,128)(2,1)S(1)} %collective-permute-done.17.refs_6_), channel_id=1, source_target_pairs={{0,28},{1,29},{2,30},{3,31},{4,0},{5,1},{6,2},{7,3},{8,4},{9,5},{1... | collective-permute-start | bytes 589832 | tf_op jit(solution)/shard_map/ppermute | solution.py:33
  73.0 5.4 %collective-permute-done.18.refs_2_ = bf16[768,128]{1,0:T(8,128)(2,1)S(1)} collective-permute-done((bf16[768,128]{1,0:T(8,128)(2,1)S(1)}, bf16[768,128]{1,0:T(8,128)(2,1)S(1)}, u32[]{:S(2)}, u32[]{:S(2)}) %collective-permute-start.18) | collective-permute-done | bytes 196640 | tf_op jit(solution)/shard_map/ppermute | solution.py:33
  78.4 3.2 %collective-permute-start.23 = (bf16[768,128]{1,0:T(8,128)(2,1)S(1)}, bf16[768,128]{1,0:T(8,128)(2,1)S(1)}, u32[]{:S(2)}, u32[]{:S(2)}) collective-permute-start(bf16[768,128]{1,0:T(8,128)(2,1)S(1)} %collective-permute-done.19.refs_3_), channel_id=1, source_target_pairs={{0,28},{1,29},{2,30},{3,31},{4,0},{5,1},{6,2},{7,3},{8,4},{9,5},{1... | collective-permute-start | bytes 589832 | tf_op jit(solution)/shard_map/ppermute | solution.py:33
  81.7 4.5 %collective-permute-done.22 = bf16[768,128]{1,0:T(8,128)(2,1)S(1)} collective-permute-done((bf16[768,128]{1,0:T(8,128)(2,1)S(1)}, bf16[768,128]{1,0:T(8,128)(2,1)S(1)}, u32[]{:S(2)}, u32[]{:S(2)}) %collective-permute-start.22) | collective-permute-done | bytes 196640 | tf_op jit(solution)/shard_map/ppermute | solution.py:33
  87.9 7.3 %collective-permute-done.24 = bf16[768,128]{1,0:T(8,128)(2,1)S(1)} collective-permute-done((bf16[768,128]{1,0:T(8,128)(2,1)S(1)}, bf16[768,128]{1,0:T(8,128)(2,1)S(1)}, u32[]{:S(2)}, u32[]{:S(2)}) %collective-permute-start.24) | collective-permute-done | bytes 196640 | tf_op jit(solution)/shard_map/ppermute | solution.py:33
  98.9 11.1 %collective-permute-done.9.refs_4_ = bf16[4,768,128]{2,1,0:T(8,128)(2,1)S(1)} collective-permute-done((bf16[4,768,128]{2,1,0:T(8,128)(2,1)S(1)}, bf16[4,768,128]{2,1,0:T(8,128)(2,1)S(1)}, u32[]{:S(2)}, u32[]{:S(2)}) %collective-permute-start.9) | collective-permute-done | bytes 786464 | tf_op jit(solution)/shard_map/ppermute | solution.py:33
  111.1 4.5 %collective-permute-done.28.refs_3_ = bf16[4,768,128]{2,1,0:T(8,128)(2,1)S(1)} collective-permute-done((bf16[4,768,128]{2,1,0:T(8,128)(2,1)S(1)}, bf16[4,768,128]{2,1,0:T(8,128)(2,1)S(1)}, u32[]{:S(2)}, u32[]{:S(2)}) %collective-permute-start.28) | collective-permute-done | bytes 786464 | tf_op jit(solution)/shard_map/ppermute | solution.py:33
  117.0 8.3 %collective-permute-done.25.refs_3_ = bf16[3,768,128]{2,1,0:T(8,128)(2,1)S(1)} collective-permute-done((bf16[3,768,128]{2,1,0:T(8,128)(2,1)S(1)}, bf16[3,768,128]{2,1,0:T(8,128)(2,1)S(1)}, u32[]{:S(2)}, u32[]{:S(2)}) %collective-permute-start.25) | collective-permute-done | bytes 589856 | tf_op jit(solution)/shard_map/ppermute | solution.py:33
  131.6 9.8 %collective-permute-done.27.refs_2_ = bf16[3,768,128]{2,1,0:T(8,128)(2,1)S(1)} collective-permute-done((bf16[3,768,128]{2,1,0:T(8,128)(2,1)S(1)}, bf16[3,768,128]{2,1,0:T(8,128)(2,1)S(1)}, u32[]{:S(2)}, u32[]{:S(2)}) %collective-permute-start.27) | collective-permute-done | bytes 589856 | tf_op jit(solution)/shard_map/ppermute | solution.py:33
  143.9 2.6 %shard_map.38 = (bf16[2,2,128,8192]{3,2,1,0:T(8,128)(2,1)}, bf16[15,2,128,128]{3,2,1,0:T(8,128)(2,1)S(1)}) custom-call(bf16[2,256,768]{2,1,0:T(8,128)(2,1)S(1)} %shard_map.32.refs_0_, bf16[2,256,768]{2,1,0:T(8,128)(2,1)S(1)} %shard_map.33.refs_1_, bf16[4,768,128]{2,1,0:T(8,128)(2,1)S(1)} %collective-permute-done.21.refs_2_, ...), custom_call_target="tpu_custom_call", output_to_operand_aliasing={{0}: (6, {})} | custom-call | flops 1509949440 | bytes 4915200 | tf_op jit(solution)/shard_map/pallas_call | solution.py:257
  146.5 3.6 %collective-permute-start.35 = (bf16[15,2,128,128]{3,2,1,0:T(8,128)(2,1)S(1)}, bf16[15,2,128,128]{3,2,1,0:T(8,128)(2,1)S(1)}, u32[]{:S(2)}, u32[]{:S(2)}) collective-permute-start(bf16[15,2,128,128]{3,2,1,0:T(8,128)(2,1)S(1)} %get-tuple-element.47), channel_id=1, source_target_pairs={{0,32},{1,33},{2,34},{3,35},{4,36},{5,37},{6,38},{7,39},{8,40},{9,... | collective-permute-start | bytes 2949128 | tf_op jit(solution)/shard_map/ppermute | solution.py:33
  150.2 3.3 %collective-permute-start.15 = (bf16[2,768,128]{2,1,0:T(8,128)(2,1)S(1)}, bf16[2,768,128]{2,1,0:T(8,128)(2,1)S(1)}, u32[]{:S(2)}, u32[]{:S(2)}) collective-permute-start(bf16[2,768,128]{2,1,0:T(8,128)(2,1)S(1)} %slice.33), channel_id=1, source_target_pairs={{0,28},{1,29},{2,30},{3,31},{4,0},{5,1},{6,2},{7,3},{8,4},{9,5},{1... | collective-permute-start | bytes 1179656 | tf_op jit(solution)/shard_map/ppermute | solution.py:33
  153.5 4.1 %collective-permute-done.31.refs_0_ = bf16[8,2,128,128]{3,2,1,0:T(8,128)(2,1)S(1)} collective-permute-done((bf16[8,2,128,128]{3,2,1,0:T(8,128)(2,1)S(1)}, bf16[8,2,128,128]{3,2,1,0:T(8,128)(2,1)S(1)}, u32[]{:S(2)}, u32[]{:S(2)}) %collective-permute-start.31) | collective-permute-done | bytes 524320 | tf_op jit(solution)/shard_map/ppermute | solution.py:33
  157.7 3.5 %collective-permute-start.33 = (bf16[8,2,128,128]{3,2,1,0:T(8,128)(2,1)S(1)}, bf16[8,2,128,128]{3,2,1,0:T(8,128)(2,1)S(1)}, u32[]{:S(2)}, u32[]{:S(2)}) collective-permute-start(bf16[8,2,128,128]{3,2,1,0:T(8,128)(2,1)S(1)} %get-tuple-element.45), channel_id=1, source_target_pairs={{0,32},{1,33},{2,34},{3,35},{4,36},{5,37},{6,38},{7,39},{8,40},{9,... | collective-permute-start | bytes 1572872 | tf_op jit(solution)/shard_map/ppermute | solution.py:33
  164.6 40.8 %collective-permute-done.32.refs_1_ = bf16[5,2,128,128]{3,2,1,0:T(8,128)(2,1)S(1)} collective-permute-done((bf16[5,2,128,128]{3,2,1,0:T(8,128)(2,1)S(1)}, bf16[5,2,128,128]{3,2,1,0:T(8,128)(2,1)S(1)}, u32[]{:S(2)}, u32[]{:S(2)}) %collective-permute-start.32) | collective-permute-done | bytes 327712 | tf_op jit(solution)/shard_map/ppermute | solution.py:33
  205.4 11.2 %collective-permute-done.33.refs_2_ = bf16[8,2,128,128]{3,2,1,0:T(8,128)(2,1)S(1)} collective-permute-done((bf16[8,2,128,128]{3,2,1,0:T(8,128)(2,1)S(1)}, bf16[8,2,128,128]{3,2,1,0:T(8,128)(2,1)S(1)}, u32[]{:S(2)}, u32[]{:S(2)}) %collective-permute-start.33) | collective-permute-done | bytes 524320 | tf_op jit(solution)/shard_map/ppermute | solution.py:33
  218.8 8.2 %collective-permute-done.30.refs_0_ = bf16[8,2,128,128]{3,2,1,0:T(8,128)(2,1)S(1)} collective-permute-done((bf16[8,2,128,128]{3,2,1,0:T(8,128)(2,1)S(1)}, bf16[8,2,128,128]{3,2,1,0:T(8,128)(2,1)S(1)}, u32[]{:S(2)}, u32[]{:S(2)}) %collective-permute-start.30) | collective-permute-done | bytes 524320 | tf_op jit(solution)/shard_map/ppermute | solution.py:33
  (76 shorter events, 44.9 us)
Async XLA Ops:
  22.0 16.8 %collective-permute-start.7 = (bf16[2,768,128]{2,1,0:T(8,128)(2,1)S(1)}, bf16[2,768,128]{2,1,0:T(8,128)(2,1)S(1)}, u32[]{:S(2)}, u32[]{:S(2)}) collective-permute-start(bf16[2,768,128]{2,1,0:T(8,128)(2,1)S(1)} %shard_map.31.feat_ref.refs_4_), channel_id=1, source_target_pairs={{0,128},{1,129},{2,130},{3,131},{4,132},{5,133},{6,134},{7,135},{8... | collective-permute-start | bytes 1179656 | tf_op jit(solution)/shard_map/ppermute | solution.py:33
  38.9 47.3 %collective-permute-start.8 = (bf16[4,768,128]{2,1,0:T(8,128)(2,1)S(1)}, bf16[4,768,128]{2,1,0:T(8,128)(2,1)S(1)}, u32[]{:S(2)}, u32[]{:S(2)}) collective-permute-start(bf16[4,768,128]{2,1,0:T(8,128)(2,1)S(1)} %pad_maximum_fusion), channel_id=1, source_target_pairs={{0,4},{1,5},{2,6},{3,7},{4,8},{5,9},{6,10},{7,11},{8,12},{9,13},{1... | collective-permute-start | bytes 2359304 | tf_op jit(solution)/shard_map/ppermute | solution.py:33
  40.1 29.6 %collective-permute-start.16 = (bf16[768,128]{1,0:T(8,128)(2,1)S(1)}, bf16[768,128]{1,0:T(8,128)(2,1)S(1)}, u32[]{:S(2)}, u32[]{:S(2)}) collective-permute-start(bf16[768,128]{1,0:T(8,128)(2,1)S(1)} %get-tuple-element.49), channel_id=1, source_target_pairs={{0,4},{1,5},{2,6},{3,7},{4,8},{5,9},{6,10},{7,11},{8,12},{9,13},{1... | collective-permute-start | bytes 589832 | tf_op jit(solution)/shard_map/ppermute | solution.py:33
  43.2 26.6 %collective-permute-start.17 = (bf16[768,128]{1,0:T(8,128)(2,1)S(1)}, bf16[768,128]{1,0:T(8,128)(2,1)S(1)}, u32[]{:S(2)}, u32[]{:S(2)}) collective-permute-start(bf16[768,128]{1,0:T(8,128)(2,1)S(1)} %get-tuple-element.49), channel_id=1, source_target_pairs={{0,28},{1,29},{2,30},{3,31},{4,0},{5,1},{6,2},{7,3},{8,4},{9,5},{1... | collective-permute-start | bytes 589832 | tf_op jit(solution)/shard_map/ppermute | solution.py:33
  48.1 47.8 %collective-permute-start.12 = (bf16[4,768,128]{2,1,0:T(8,128)(2,1)S(1)}, bf16[4,768,128]{2,1,0:T(8,128)(2,1)S(1)}, u32[]{:S(2)}, u32[]{:S(2)}) collective-permute-start(bf16[4,768,128]{2,1,0:T(8,128)(2,1)S(1)} %pad_maximum_fusion), channel_id=1, source_target_pairs={{0,28},{1,29},{2,30},{3,31},{4,0},{5,1},{6,2},{7,3},{8,4},{9,5},{1... | collective-permute-start | bytes 2359304 | tf_op jit(solution)/shard_map/ppermute | solution.py:33
  86.2 23.8 %collective-permute-start.9 = (bf16[4,768,128]{2,1,0:T(8,128)(2,1)S(1)}, bf16[4,768,128]{2,1,0:T(8,128)(2,1)S(1)}, u32[]{:S(2)}, u32[]{:S(2)}) collective-permute-start(bf16[4,768,128]{2,1,0:T(8,128)(2,1)S(1)} %collective-permute-done.8.refs_4_), channel_id=1, source_target_pairs={{0,4},{1,5},{2,6},{3,7},{4,8},{5,9},{6,10},{7,11},{8,12},{9,13},{1... | collective-permute-start | bytes 2359304 | tf_op jit(solution)/shard_map/ppermute | solution.py:33
  86.4 23.6 %collective-permute-start.20 = (bf16[4,768,128]{2,1,0:T(8,128)(2,1)S(1)}, bf16[4,768,128]{2,1,0:T(8,128)(2,1)S(1)}, u32[]{:S(2)}, u32[]{:S(2)}) collective-permute-start(bf16[4,768,128]{2,1,0:T(8,128)(2,1)S(1)} %pad_maximum_fusion.1), channel_id=1, source_target_pairs={{0,64},{1,65},{2,66},{3,67},{4,68},{5,69},{6,70},{7,71},{8,72},{9,... | collective-permute-start | bytes 2359304 | tf_op jit(solution)/shard_map/ppermute | solution.py:33
  95.2 20.4 %collective-permute-start.28 = (bf16[4,768,128]{2,1,0:T(8,128)(2,1)S(1)}, bf16[4,768,128]{2,1,0:T(8,128)(2,1)S(1)}, u32[]{:S(2)}, u32[]{:S(2)}) collective-permute-start(bf16[4,768,128]{2,1,0:T(8,128)(2,1)S(1)} %pad_maximum_fusion.1), channel_id=1, source_target_pairs={{0,192},{1,193},{2,194},{3,195},{4,196},{5,197},{6,198},{7,199},{8... | collective-permute-start | bytes 2359304 | tf_op jit(solution)/shard_map/ppermute | solution.py:33
  96.0 30.3 %collective-permute-start.13 = (bf16[4,768,128]{2,1,0:T(8,128)(2,1)S(1)}, bf16[4,768,128]{2,1,0:T(8,128)(2,1)S(1)}, u32[]{:S(2)}, u32[]{:S(2)}) collective-permute-start(bf16[4,768,128]{2,1,0:T(8,128)(2,1)S(1)} %collective-permute-done.12.refs_5_), channel_id=1, source_target_pairs={{0,28},{1,29},{2,30},{3,31},{4,0},{5,1},{6,2},{7,3},{8,4},{9,5},{1... | collective-permute-start | bytes 2359304 | tf_op jit(solution)/shard_map/ppermute | solution.py:33
  97.6 27.7 %collective-permute-start.25 = (bf16[3,768,128]{2,1,0:T(8,128)(2,1)S(1)}, bf16[3,768,128]{2,1,0:T(8,128)(2,1)S(1)}, u32[]{:S(2)}, u32[]{:S(2)}) collective-permute-start(bf16[3,768,128]{2,1,0:T(8,128)(2,1)S(1)} %pad_maximum_fusion.2.refs_4_), channel_id=1, source_target_pairs={{0,192},{1,193},{2,194},{3,195},{4,196},{5,197},{6,198},{7,199},{8... | collective-permute-start | bytes 1769480 | tf_op jit(solution)/shard_map/ppermute | solution.py:33
  110.0 33.7 %collective-permute-start.10 = (bf16[4,768,128]{2,1,0:T(8,128)(2,1)S(1)}, bf16[4,768,128]{2,1,0:T(8,128)(2,1)S(1)}, u32[]{:S(2)}, u32[]{:S(2)}) collective-permute-start(bf16[4,768,128]{2,1,0:T(8,128)(2,1)S(1)} %collective-permute-done.9.refs_4_), channel_id=1, source_target_pairs={{0,4},{1,5},{2,6},{3,7},{4,8},{5,9},{6,10},{7,11},{8,12},{9,13},{1... | collective-permute-start | bytes 2359304 | tf_op jit(solution)/shard_map/ppermute | solution.py:33
  110.0 33.9 %collective-permute-start.21 = (bf16[4,768,128]{2,1,0:T(8,128)(2,1)S(1)}, bf16[4,768,128]{2,1,0:T(8,128)(2,1)S(1)}, u32[]{:S(2)}, u32[]{:S(2)}) collective-permute-start(bf16[4,768,128]{2,1,0:T(8,128)(2,1)S(1)} %collective-permute-done.20.refs_2_), channel_id=1, source_target_pairs={{0,64},{1,65},{2,66},{3,67},{4,68},{5,69},{6,70},{7,71},{8,72},{9,... | collective-permute-start | bytes 2359304 | tf_op jit(solution)/shard_map/ppermute | solution.py:33
  115.6 25.8 %collective-permute-start.27 = (bf16[3,768,128]{2,1,0:T(8,128)(2,1)S(1)}, bf16[3,768,128]{2,1,0:T(8,128)(2,1)S(1)}, u32[]{:S(2)}, u32[]{:S(2)}) collective-permute-start(bf16[3,768,128]{2,1,0:T(8,128)(2,1)S(1)} %pad_maximum_fusion.2.refs_4_), channel_id=1, source_target_pairs={{0,64},{1,65},{2,66},{3,67},{4,68},{5,69},{6,70},{7,71},{8,72},{9,... | collective-permute-start | bytes 1769480 | tf_op jit(solution)/shard_map/ppermute | solution.py:33
  125.4 18.5 %collective-permute-start.26 = (bf16[3,768,128]{2,1,0:T(8,128)(2,1)S(1)}, bf16[3,768,128]{2,1,0:T(8,128)(2,1)S(1)}, u32[]{:S(2)}, u32[]{:S(2)}) collective-permute-start(bf16[3,768,128]{2,1,0:T(8,128)(2,1)S(1)} %collective-permute-done.25.refs_3_), channel_id=1, source_target_pairs={{0,192},{1,193},{2,194},{3,195},{4,196},{5,197},{6,198},{7,199},{8... | collective-permute-start | bytes 1769480 | tf_op jit(solution)/shard_map/ppermute | solution.py:33
  126.3 23.9 %collective-permute-start.14 = (bf16[4,768,128]{2,1,0:T(8,128)(2,1)S(1)}, bf16[4,768,128]{2,1,0:T(8,128)(2,1)S(1)}, u32[]{:S(2)}, u32[]{:S(2)}) collective-permute-start(bf16[4,768,128]{2,1,0:T(8,128)(2,1)S(1)} %collective-permute-done.13.refs_5_), channel_id=1, source_target_pairs={{0,28},{1,29},{2,30},{3,31},{4,0},{5,1},{6,2},{7,3},{8,4},{9,5},{1... | collective-permute-start | bytes 2359304 | tf_op jit(solution)/shard_map/ppermute | solution.py:33
  141.3 16.3 %collective-permute-start.31 = (bf16[8,2,128,128]{3,2,1,0:T(8,128)(2,1)S(1)}, bf16[8,2,128,128]{3,2,1,0:T(8,128)(2,1)S(1)}, u32[]{:S(2)}, u32[]{:S(2)}) collective-permute-start(bf16[8,2,128,128]{3,2,1,0:T(8,128)(2,1)S(1)} %get-tuple-element.43), channel_id=1, source_target_pairs={{0,32},{1,33},{2,34},{3,35},{4,36},{5,37},{6,38},{7,39},{8,40},{9,... | collective-permute-start | bytes 1572872 | tf_op jit(solution)/shard_map/ppermute | solution.py:33
  143.8 13.9 %collective-permute-start.11 = (bf16[2,768,128]{2,1,0:T(8,128)(2,1)S(1)}, bf16[2,768,128]{2,1,0:T(8,128)(2,1)S(1)}, u32[]{:S(2)}, u32[]{:S(2)}) collective-permute-start(bf16[2,768,128]{2,1,0:T(8,128)(2,1)S(1)} %slice.32), channel_id=1, source_target_pairs={{0,4},{1,5},{2,6},{3,7},{4,8},{5,9},{6,10},{7,11},{8,12},{9,13},{1... | collective-permute-start | bytes 1179656 | tf_op jit(solution)/shard_map/ppermute | solution.py:33
  146.5 70.2 %collective-permute-start.35 = (bf16[15,2,128,128]{3,2,1,0:T(8,128)(2,1)S(1)}, bf16[15,2,128,128]{3,2,1,0:T(8,128)(2,1)S(1)}, u32[]{:S(2)}, u32[]{:S(2)}) collective-permute-start(bf16[15,2,128,128]{3,2,1,0:T(8,128)(2,1)S(1)} %get-tuple-element.47), channel_id=1, source_target_pairs={{0,32},{1,33},{2,34},{3,35},{4,36},{5,37},{6,38},{7,39},{8,40},{9,... | collective-permute-start | bytes 2949128 | tf_op jit(solution)/shard_map/ppermute | solution.py:33
  150.1 66.5 %collective-permute-start.34 = (bf16[14,2,128,128]{3,2,1,0:T(8,128)(2,1)S(1)}, bf16[14,2,128,128]{3,2,1,0:T(8,128)(2,1)S(1)}, u32[]{:S(2)}, u32[]{:S(2)}) collective-permute-start(bf16[14,2,128,128]{3,2,1,0:T(8,128)(2,1)S(1)} %get-tuple-element.46), channel_id=1, source_target_pairs={{0,32},{1,33},{2,34},{3,35},{4,36},{5,37},{6,38},{7,39},{8,40},{9,... | collective-permute-start | bytes 2752520 | tf_op jit(solution)/shard_map/ppermute | solution.py:33
  150.2 12.9 %collective-permute-start.15 = (bf16[2,768,128]{2,1,0:T(8,128)(2,1)S(1)}, bf16[2,768,128]{2,1,0:T(8,128)(2,1)S(1)}, u32[]{:S(2)}, u32[]{:S(2)}) collective-permute-start(bf16[2,768,128]{2,1,0:T(8,128)(2,1)S(1)} %slice.33), channel_id=1, source_target_pairs={{0,28},{1,29},{2,30},{3,31},{4,0},{5,1},{6,2},{7,3},{8,4},{9,5},{1... | collective-permute-start | bytes 1179656 | tf_op jit(solution)/shard_map/ppermute | solution.py:33
  157.6 47.8 %collective-permute-start.32 = (bf16[5,2,128,128]{3,2,1,0:T(8,128)(2,1)S(1)}, bf16[5,2,128,128]{3,2,1,0:T(8,128)(2,1)S(1)}, u32[]{:S(2)}, u32[]{:S(2)}) collective-permute-start(bf16[5,2,128,128]{3,2,1,0:T(8,128)(2,1)S(1)} %get-tuple-element.44), channel_id=1, source_target_pairs={{0,32},{1,33},{2,34},{3,35},{4,36},{5,37},{6,38},{7,39},{8,40},{9,... | collective-permute-start | bytes 983048 | tf_op jit(solution)/shard_map/ppermute | solution.py:33
  157.7 59.0 %collective-permute-start.33 = (bf16[8,2,128,128]{3,2,1,0:T(8,128)(2,1)S(1)}, bf16[8,2,128,128]{3,2,1,0:T(8,128)(2,1)S(1)}, u32[]{:S(2)}, u32[]{:S(2)}) collective-permute-start(bf16[8,2,128,128]{3,2,1,0:T(8,128)(2,1)S(1)} %get-tuple-element.45), channel_id=1, source_target_pairs={{0,32},{1,33},{2,34},{3,35},{4,36},{5,37},{6,38},{7,39},{8,40},{9,... | collective-permute-start | bytes 1572872 | tf_op jit(solution)/shard_map/ppermute | solution.py:33
  163.2 63.7 %collective-permute-start.30 = (bf16[8,2,128,128]{3,2,1,0:T(8,128)(2,1)S(1)}, bf16[8,2,128,128]{3,2,1,0:T(8,128)(2,1)S(1)}, u32[]{:S(2)}, u32[]{:S(2)}) collective-permute-start(bf16[8,2,128,128]{3,2,1,0:T(8,128)(2,1)S(1)} %get-tuple-element.42), channel_id=1, source_target_pairs={{0,32},{1,33},{2,34},{3,35},{4,36},{5,37},{6,38},{7,39},{8,40},{9,... | collective-permute-start | bytes 1572872 | tf_op jit(solution)/shard_map/ppermute | solution.py:33
  205.4 24.3 %collective-permute-start.29 = (bf16[4,2,128,128]{3,2,1,0:T(8,128)(2,1)S(1)}, bf16[4,2,128,128]{3,2,1,0:T(8,128)(2,1)S(1)}, u32[]{:S(2)}, u32[]{:S(2)}) collective-permute-start(bf16[4,2,128,128]{3,2,1,0:T(8,128)(2,1)S(1)} %get-tuple-element.41), channel_id=1, source_target_pairs={{0,32},{1,33},{2,34},{3,35},{4,36},{5,37},{6,38},{7,39},{8,40},{9,... | collective-permute-start | bytes 786440 | tf_op jit(solution)/shard_map/ppermute | solution.py:33
  (12 other events, 101.1 us)
